TPU v7x, 128 devices: a whole 4x4x4 slice. The times are simulated.
128 devices in a mesh: seq: 32 (over y, x, core), hid: 4 (over z).
Axes of the slice: x: 4, y: 4, z: 4, core: 2. Of those that a mesh axis runs over, the one named last changes fastest.
Arguments:
- patches: bfloat16 [12288, 3200], P('seq'), may hold values from -6 to 6
- norm_gain: float32 [3200], replicated, may hold values from 0.5 to 8
- query_weight: bfloat16 [3200, 2048], P(None, 'hid'), may hold values from -0.109375 to 0.109375
- key_weight: bfloat16 [3200, 2048], P(None, 'hid'), may hold values from -0.7424621 to 0.7424621
- value_weight: bfloat16 [3200, 2048], P(None, 'hid'), may hold values from -0.109375 to 0.109375
- out_weight: bfloat16 [2048, 3200], P('hid'), may hold values from -0.125 to 0.125
- layer_scale: float32 [3200], replicated, may hold values from 0.3 to 1.5
- merge_gain: float32 [12800], P('hid'), may hold values from 0.5 to 1.5
- merge_bias: float32 [12800], P('hid'), may hold values from -3 to 3
- proj_weight: bfloat16 [12800, 6144], P('hid', 'seq'), may hold values from -0.0546875 to 0.0546875
- proj_bias: float32 [6144], P('seq'), may hold values from -3 to 3
- text_rows: bfloat16 [512, 6144], P(None, 'seq'), may hold values from -6 to 6
- stream_gain: float32 [6144], P('hid'), may hold values from 0.5 to 1.5
- tile_counts: int32 [3], replicated, may hold values from 1 to 7, as said below
- image_slots: int32 [3072], replicated, may hold values from 0 to 3583, as said below
- text_slots: int32 [512], replicated, may hold values from 0 to 3583, as said below
Outputs:
- stream: bfloat16 [3584, 6144], P('seq', 'hid')
- normed: bfloat16 [3584, 6144], P('seq', 'hid')
Inputs may be any that keep to these rules, and one draw needn't show every extreme that they name: `tile_counts`: the tile counts sum to 12; the largest is exactly 7. `image_slots`: image slots and text slots together name every stream position once; each image's rows lie in order at consecutive positions. `text_slots`: see image_slots; text slots increase.
All inputs are finite; a program needn't handle non-finite values.
Results may differ from a plain program's by a relative error of at most 0.022.
The roundings to bfloat16 on the way count: a program that leaves them out, or rounds other values in their place, can miss the bound.
Values may be sent and summed in bfloat16 or wider, within the bound.
No kernel may reach another device: no remote copies, remote signals or barrier semaphores. Data moves between devices by JAX's collectives and lax.ppermute only.
A program may use at most 192 MiB of HBM per device.

v0:
```python
import jax
import jax.numpy as jnp
from jax import lax
from jax.experimental import pallas as pl
from jax.experimental.pallas import tpu as pltpu
from jax.sharding import Mesh, PartitionSpec as P

HD = 128
ROWS = 384
MROWS = 96
BF = jnp.bfloat16
F32 = jnp.float32
LIMIT = 60 * 1024 * 1024


def cdot(a, b):
    return jnp.dot(a, b, preferred_element_type=F32)


def shift(value, axis, k):
    return lax.ppermute(value, axis, [(i, (i + k) % 4) for i in range(4)])


def swap(value):
    return lax.ppermute(value, "c", [(0, 1), (1, 0)])


def cost(us):
    return pl.CostEstimate(flops=int(us * 1.0e9), transcendentals=0, bytes_accessed=0)


def call(body, out_shape, us, scratch=(), **kw):
    return pl.pallas_call(
        body,
        out_shape=out_shape,
        scratch_shapes=scratch,
        cost_estimate=cost(us),
        compiler_params=pltpu.CompilerParams(vmem_limit_bytes=LIMIT),
        **kw,
    )


SMEM = pl.BlockSpec(memory_space=pltpu.SMEM)
VMEM = pl.BlockSpec(memory_space=pltpu.VMEM)
ANY = pl.BlockSpec(memory_space=pl.ANY)


def sub_row_permutation():
    row = lax.broadcasted_iota(jnp.int32, (ROWS, ROWS), 0)
    col = lax.broadcasted_iota(jnp.int32, (ROWS, ROWS), 1)
    sub = (row >= 96).astype(jnp.int32) + (row >= 192).astype(jnp.int32) + (row >= 288).astype(jnp.int32)
    m = row - 96 * sub
    source = (2 * (m >> 4) + (sub >> 1)) * 32 + 2 * (m & 15) + (sub & 1)
    return jnp.where(source == col, 1.0, 0.0).astype(BF)


def qkv_body(s_ref, x_ref, g_ref, wk_ref, wv_ref, wq_ref, o0, o1, o2, o3, xn_ref):
    half = pl.program_id(0)

    @pl.when(half == 0)
    def _():
        xf = cdot(sub_row_permutation(), x_ref[...])
        scale = lax.rsqrt(jnp.mean(xf * xf, axis=-1, keepdims=True) + 1e-06)
        gain = jnp.concatenate([g_ref[i : i + 1] for i in range(g_ref.shape[0])], axis=1)
        xn_ref[...] = (xf * scale * gain).astype(BF)

    xn = xn_ref[...]
    keys = cdot(xn, wk_ref[...]).astype(BF)
    values = cdot(xn, wv_ref[...]).astype(BF)
    queries = (cdot(xn, wq_ref[...]) * HD ** (-0.5)).astype(BF)
    for i in range(2):
        slot = (2 * half + i - s_ref[0]) & 3
        part = slice(HD * i, HD * (i + 1))
        head = jnp.concatenate([keys[:, part], values[:, part], queries[:, part]], axis=1)
        for k, ref in enumerate((o0, o1, o2, o3)):

            @pl.when(slot == k)
            def _(ref=ref, head=head):
                ref[...] = head


def project_qkv(y, patches, gain, wk, wv, wq):
    width = patches.shape[1]
    whole = pl.BlockSpec((ROWS, width), lambda j, s: (0, 0))
    weight = pl.BlockSpec((width, 2 * HD), lambda j, s: (0, j))
    return pl.pallas_call(
        qkv_body,
        out_shape=[jax.ShapeDtypeStruct((ROWS, 3 * HD), BF)] * 4,
        grid_spec=pltpu.PrefetchScalarGridSpec(
            num_scalar_prefetch=1,
            grid=(2,),
            in_specs=[whole, pl.BlockSpec((width // HD, HD), lambda j, s: (0, 0)), weight, weight, weight],
            out_specs=[pl.BlockSpec((ROWS, 3 * HD), lambda j, s: (0, 0))] * 4,
            scratch_shapes=[pltpu.VMEM((ROWS, width), BF)],
        ),
        cost_estimate=cost(11),
        compiler_params=pltpu.CompilerParams(
            dimension_semantics=("arbitrary",), vmem_limit_bytes=LIMIT
        ),
    )(y, patches, gain, wk, wv, wq)


def image_lanes(info, scale, same):
    row = lax.broadcasted_iota(jnp.int32, (ROWS, HD), 0)
    lane = lax.broadcasted_iota(jnp.int32, (ROWS, HD), 1)
    sub = (row >= 96).astype(jnp.int32) + (row >= 192).astype(jnp.int32) + (row >= 288).astype(jnp.int32)
    image = jnp.where((row - 96 * sub) * 4 < info[2], info[0], info[1])
    hit = lane == image if same else lane != image
    return jnp.where(hit, scale, 0.0).astype(BF)


def attention_body(steps, first, last, s_ref, t_ref, q_ref, *refs):
    rest = refs[:-3]
    own_ref, sib_ref, list_ref = refs[-3:]
    filled = 0
    while filled < len(steps):
        own, sib = rest[:2]
        rest = rest[2:]
        own_ref[filled : filled + own.shape[0]] = own[...]
        sib_ref[filled : filled + own.shape[0]] = sib[...]
        filled += own.shape[0]
    if not first:
        acc_in, max_in = rest[:2]
        rest = rest[2:]
    if last:
        *o_refs, acc_ref, max_ref = rest
    else:
        acc_ref, max_ref = rest
    if first:
        acc_ref[...] = jnp.zeros(acc_ref.shape, F32)
        max_ref[...] = jnp.full(max_ref.shape, -1e30, F32)
    else:
        acc_ref[...] = acc_in[...]
        max_ref[...] = max_in[...]
    y, x, c = s_ref[0], s_ref[1], s_ref[2]
    bound0 = 1024 * t_ref[0]
    bound1 = 1024 * (t_ref[0] + t_ref[1])

    def image_of(row):
        return (row >= bound0).astype(jnp.int32) + (row >= bound1).astype(jnp.int32)

    def block(yy, xx, cc):
        base = ROWS * (8 * yy + 2 * xx + cc)
        return image_of(base), image_of(base + ROWS - 1), 1024 - (base & 1023)

    def blocks_of(i):
        qb = i & 3
        kr = i >> 2
        step = steps[0] if len(steps) == 4 else jnp.where(kr < 4, steps[0], steps[4])
        xk = (x - step) & 3
        ki = [block((y - kr) & 3, xk, cc) for cc in (c, 1 - c)]
        return qb, kr, block((y - qb) & 3, x, c), ki

    def note(i, count):
        qb, kr, qi, ki = blocks_of(i)
        low = jnp.minimum(ki[0][0], ki[1][0])
        high = jnp.maximum(ki[0][1], ki[1][1])
        meets = jnp.logical_and(qi[1] >= low, qi[0] <= high)
        list_ref[count] = i
        return count + meets.astype(jnp.int32)

    def score(i, live):
        qb, kr, qi, ki = blocks_of(i)
        qi = (jnp.where(live, qi[0], 99), jnp.where(live, qi[1], 99), qi[2])
        q = jnp.concatenate([q_ref[qb], image_lanes(qi, -1e30, False)], axis=1)
        keys, values = [], []
        for n, ref in enumerate((own_ref, sib_ref)):
            keys.append(jnp.concatenate([ref[kr, :, 0:HD], image_lanes(ki[n], 1.0, True)], axis=1))
            values.append(
                jnp.concatenate([ref[kr, :, HD : 2 * HD], jnp.ones((ROWS, HD), BF)], axis=1)
            )
        scores = lax.dot_general(
            q, jnp.concatenate(keys, axis=0), (((1,), (1,)), ((), ())), preferred_element_type=F32
        )
        return qb, scores, jnp.concatenate(values, axis=0)

    def fold(qb, scores, values):
        old = max_ref[qb]
        new = jnp.maximum(old, jnp.max(scores, axis=1, keepdims=True))
        factor = jnp.exp(old - new)
        weights = jnp.exp(scores - new[:, 0:1]).astype(BF)
        max_ref[qb] = new
        acc_ref[qb] = acc_ref[qb] * jnp.concatenate([factor, factor], axis=1) + cdot(weights, values)

    def alone(t, carry):
        fold(*score(list_ref[t], True))
        return carry

    def two(t, carry):
        odd = 2 * t + 1 < count
        one = score(list_ref[2 * t], True)
        other = score(list_ref[jnp.where(odd, 2 * t + 1, 2 * t)], odd)
        fold(*one)
        fold(*other)
        return carry

    count = lax.fori_loop(0, 4 * len(steps), note, jnp.int32(0))
    if first:
        lax.fori_loop(0, count, alone, 0)
    else:
        lax.fori_loop(0, (count + 1) >> 1, two, 0)
    if last:
        for b in range(4):
            o_refs[b][...] = (acc_ref[b, :, 0:HD] / acc_ref[b, :, HD : 2 * HD]).astype(BF)


def attend(steps, coords, tile_counts, q, blocks, state, last):
    first = state is None
    state_shapes = [
        jax.ShapeDtypeStruct((4, ROWS, 2 * HD), F32),
        jax.ShapeDtypeStruct((4, ROWS, HD), F32),
    ]
    args = [coords, tile_counts, q, *blocks] + ([] if first else list(state))

    def body(*refs):
        attention_body(steps, first, last, *refs)

    specs = [SMEM, SMEM] + [VMEM] * (len(args) - 2)
    held = [pltpu.VMEM((len(steps), ROWS, 2 * HD), BF)] * 2 + [pltpu.SMEM((64,), jnp.int32)]
    if last:
        return call(
            body,
            [jax.ShapeDtypeStruct((ROWS, HD), BF)] * 4,
            2.5 * len(steps),
            scratch=[pltpu.VMEM(s.shape, s.dtype) for s in state_shapes] + held,
            in_specs=specs,
        )(*args)
    return call(body, state_shapes, 2.5 * len(steps), scratch=held, in_specs=specs)(*args)


def pack_body(m0, m1, m2, m3, kv_ref, q_ref):
    for k, ref in enumerate((m0, m1, m2, m3)):
        kv_ref[k] = ref[:, 0 : 2 * HD]
        q_ref[k] = ref[:, 2 * HD : 3 * HD]


def turn_body(gain_ref, bias_ref, out_ref):
    out_ref[0:4] = gain_ref[...].T
    out_ref[4:8] = bias_ref[...].T


WINDOW = 896


def window(z):
    return pl.ds(pl.multiple_of(768 * z, HD), WINDOW)


def window_body(s_ref, w_ref, out_ref):
    half = out_ref.shape[1]
    rows = pl.ds(pl.multiple_of(half * s_ref[2], 64), half)
    for i in range(4):
        out_ref[i] = w_ref[rows, 768 * i : 768 * i + WINDOW]


def out_body(s_ref, o0, o1, o2, o3, mine, other, x_any, scale_ref, r_ref, stats_ref, w_ref, x_ref, sems):
    y, c, z = s_ref[0], s_ref[2], s_ref[3]
    half = mine.shape[1]
    upper = pl.ds(pl.multiple_of(half * c, 64), half)
    lower = pl.ds(pl.multiple_of(half * (1 - c), 64), half)
    copies = [
        pltpu.make_async_copy(mine, w_ref.at[:, upper], sems.at[0]),
        pltpu.make_async_copy(other, w_ref.at[:, lower], sems.at[1]),
        pltpu.make_async_copy(x_any.at[:, window(z)], x_ref, sems.at[2]),
    ]
    for copy in copies:
        copy.start()
    acc = jnp.zeros((ROWS, WINDOW), F32)
    for copy in copies:
        copy.wait()
    parts = [
        [o0[k] for k in range(4)],
        [o1[k] for k in range(4)],
        [o2[k] for k in range(4)],
        [o3[k] for k in range(4)],
    ]
    for j in range(4):
        heads = jnp.concatenate(parts[j], axis=1)
        plane = (z - j) & 3
        rows = jnp.concatenate(
            [w_ref[plane, pl.ds(pl.multiple_of(HD * ((y + k) & 3), HD), HD), :] for k in range(4)],
            axis=0,
        )
        acc = acc + cdot(heads, rows)
    residual = cdot(sub_row_permutation(), x_ref[...]) + scale_ref[:, window(z)] * acc
    residual = pltpu.roll(residual, WINDOW - 32 * z, 1)[:, 0 : r_ref.shape[2]]
    total = jnp.zeros((MROWS, 1), F32)
    squares = jnp.zeros((MROWS, 1), F32)
    for sub in range(4):
        part = residual[MROWS * sub : MROWS * (sub + 1)]
        r_ref[sub] = part
        total = total + jnp.sum(part, axis=1, keepdims=True)
        squares = squares + jnp.sum(part * part, axis=1, keepdims=True)
    lane = lax.broadcasted_iota(jnp.int32, (MROWS, HD), 1)
    stats_ref[...] = jnp.where(lane == 0, total, squares)


def interleave(parts):
    count = parts[0].shape[1]
    row = lax.broadcasted_iota(jnp.int32, (4 * count, 4 * count), 0)
    col = lax.broadcasted_iota(jnp.int32, (4 * count, 4 * count), 1)
    hit = row == (col & 3) * count + (col >> 2)
    return cdot(jnp.concatenate(parts, axis=1), jnp.where(hit, 1.0, 0.0).astype(BF)).astype(BF)


def merge_body(s0, s1, s2, s3, r_ref, affine_ref, out_ref):
    share = r_ref.shape[2]
    stats = ((s0[...] + s2[...]) + (s1[...] + s3[...])) * (1.0 / (16 * share))
    mean = stats[:, 0:1]
    scale = lax.rsqrt(stats[:, 1:2] - mean * mean + 1e-05)
    normed = []
    for sub in range(4):
        gain, bias = affine_ref[sub : sub + 1], affine_ref[4 + sub : 5 + sub]
        normed.append(((r_ref[sub] - mean) * scale * gain + bias).astype(BF))
    for start in range(0, share, HD):
        stop = min(start + HD, share)
        out_ref[:, 4 * start : 4 * stop] = interleave([n[:, start:stop] for n in normed])


def projection_body(s_ref, *refs):
    merged = refs[:10]
    weights = refs[10:17]
    outs = refs[17:21]
    a_ref, w_ref = refs[21:]
    y, x, c, z = s_ref[0], s_ref[1], s_ref[2], s_ref[3]
    for n, core in ((0, c), (5, 1 - c)):
        for part, (j, offset) in enumerate(((0, 0), (1, 0), (2, 0), (2, 48), (3, 0))):
            ref = merged[n + part]
            start = pl.multiple_of(ROWS * core + MROWS * ((x - j) & 3) + offset, 16)
            a_ref[pl.ds(start, ref.shape[0]), :] = ref[...]
    for ref, (j, offset) in zip(weights, ((0, 0), (1, 0), (1, 96), (2, 0), (2, 96), (3, 0), (3, 96))):
        start = pl.multiple_of(192 * ((y - j - z) & 3) + offset, 32)
        w_ref[pl.ds(start, ref.shape[0]), :] = ref[...]

    def rows_block(i, carry):
        rows = pl.ds(pl.multiple_of(192 * i, 64), 192)
        lower = pl.ds(pl.multiple_of(192 * i + ROWS, 64), 192)
        values = jnp.concatenate([a_ref[rows, :], a_ref[lower, :]], axis=0)
        acc = lax.dot_general(
            values, w_ref[...], (((1,), (1,)), ((), ())), preferred_element_type=F32
        )
        for n in range(4):
            block = acc[:, 192 * n : 192 * (n + 1)]
            packed = jnp.concatenate([block[0:192], block[192:ROWS]], axis=1)
            outs[n][rows, :] = packed.astype(outs[n].dtype)
        return carry

    lax.fori_loop(0, 2, rows_block, 0)


def place_body(s_ref, r0, r1, r2, r3, slots_ref, text_ref, tslots_ref, own_ref, sib_ref, rows_ref, both_ref):
    y, x, c = s_ref[0], s_ref[1], s_ref[2]

    def positions(core):
        row = lax.broadcasted_iota(jnp.int32, (448, 1), 0)
        k = (row >= 112).astype(jnp.int32) + (row >= 224).astype(jnp.int32) + (row >= 336).astype(jnp.int32)
        return 112 * (8 * y + 2 * ((x + k) & 3) + core) + row - 112 * k

    def pick(position, slots):
        return jnp.where(position == slots, 1.0, 0.0).astype(BF)

    for k, r in enumerate((r0, r1, r2, r3)):
        start = pl.multiple_of(ROWS * ((y - k) & 3), ROWS)
        both = r[...]
        rows_ref[pl.ds(start, r.shape[0]), :] = both[:, 0:192]
        rows_ref[pl.ds(4 * ROWS + start, r.shape[0]), :] = both[:, 192:384]

    def core_block(n, carry):
        where = positions(jnp.where(n == 0, c, 1 - c))
        value = cdot(pick(where, slots_ref[...]), rows_ref[...])
        value = value + cdot(pick(where, tslots_ref[...]), text_ref[...])
        both_ref[n] = value.astype(BF)
        return carry

    lax.fori_loop(0, 2, core_block, 0)
    own_ref[...] = both_ref[0]
    sib_ref[...] = both_ref[1]


def stream_body(s_ref, b0, b1, b2, b3, out_ref, squares_ref):
    x, c = s_ref[1], s_ref[2]
    width = b0.shape[1]
    total = jnp.zeros((b0.shape[0], 1), F32)
    blocks = [b0[...], b1[...], b2[...], b3[...]]
    for place in range(4):
        k = (x - place) & 3
        value = blocks[0]
        for n in range(1, 4):
            value = jnp.where(k == n, blocks[n], value)
        turned = jnp.concatenate([value[:, 192:384], value[:, 0:192]], axis=1)
        value = jnp.where(c == 0, value, turned)
        out_ref[:, width * place : width * (place + 1)] = value
        wide = value.astype(F32)
        total = total + jnp.sum(wide * wide, axis=1, keepdims=True)
    squares_ref[...] = jnp.broadcast_to(total, squares_ref.shape)


def after(values):
    return lax.optimization_barrier(values)


def over_z(value):
    return [value] + [shift(value, "z", k) for k in (1, 2, 3)]


def ring(value, axis):
    half = value.shape[0] // 2
    back = shift(value, axis, 1)
    ahead = shift(value, axis, 3)
    return [value, back, shift(back[:half], axis, 1), shift(ahead[half:], axis, 3), ahead]


def per_device(
    patches,
    norm_gain,
    query_weight,
    key_weight,
    value_weight,
    out_weight,
    layer_scale,
    merge_gain,
    merge_bias,
    proj_weight,
    proj_bias,
    text_rows,
    stream_gain,
    tile_counts,
    image_slots,
    text_slots,
):
    y, x, c, z = [lax.axis_index(name).astype(jnp.int32) for name in ("y", "x", "c", "z")]
    coords = jnp.stack([y, x, c, z])
    width = patches.shape[1]
    share = width // 4

    kvq = project_qkv(coords, patches, norm_gain.reshape(width // HD, HD), key_weight, value_weight, query_weight)

    kvq, out_weight = after((kvq, out_weight))
    moved = [kvq[0]] + [shift(kvq[k], "y", k) for k in (1, 2, 3)]
    kv_own, q_own = call(
        pack_body,
        (
            jax.ShapeDtypeStruct((4, ROWS, 2 * HD), BF),
            jax.ShapeDtypeStruct((4, ROWS, HD), BF),
        ),
        1,
        in_specs=[VMEM] * 4,
    )(*moved)
    kv_own, q_own, proj_turned = after((kv_own, q_own, proj_weight.T))
    proj_low, proj_high = proj_turned[0:96], proj_turned[96:192]
    back_low, ahead_high = shift(proj_low, "y", 1), shift(proj_high, "y", 3)
    near = [shift(kv_own, "x", 1), shift(kv_own, "x", 3)]
    kv_sib = swap(kv_own)

    where = (coords, tile_counts, q_own)
    state = attend((0,) * 4, *where, [kv_own, kv_sib], None, False)
    out_weight, state = after((out_weight, state))
    windows = call(
        window_body,
        jax.ShapeDtypeStruct((4, out_weight.shape[0] // 2, WINDOW), BF),
        0.1,
        in_specs=[SMEM, VMEM],
    )(coords, out_weight)
    near, state, windows, back_low, ahead_high, proj_low, proj_high, kv_here = after(
        (near, state, windows, back_low, ahead_high, proj_low, proj_high, kv_own)
    )
    back_high, ahead_low = shift(proj_high, "y", 1), shift(proj_low, "y", 3)
    out_half = lax.all_to_all(windows, "z", 0, 0, tiled=True)
    far = shift(kv_here, "x", 2)
    blocks = [near[0], swap(near[0]), near[1], swap(near[1])]
    state = attend((1,) * 4 + (3,) * 4, *where, blocks, state, False)
    far, state, out_half, back_low, ahead_high, back_high, ahead_low = after(
        (far, state, out_half, back_low, ahead_high, back_high, ahead_low)
    )
    proj_parts = [
        proj_turned,
        back_low,
        back_high,
        shift(back_low, "y", 1),
        shift(ahead_high, "y", 3),
        ahead_low,
        ahead_high,
    ]
    attended = attend((2,) * 4, *where, [far, swap(far)], state, True)
    heads = jnp.stack([attended[0]] + [shift(attended[k], "y", 4 - k) for k in (1, 2, 3)])
    heads, merge_gain, merge_bias, layer_scale, text_rows, proj_bias, proj_parts, out_half = after(
        (heads, merge_gain, merge_bias, layer_scale, text_rows, proj_bias, proj_parts, out_half)
    )

    head_parts = [heads] + [shift(heads, "z", k) for k in (1, 2, 3)]
    affine = call(
        turn_body, jax.ShapeDtypeStruct((8, share), F32), 1, in_specs=[VMEM] * 2
    )(merge_gain.reshape(share, 4), merge_bias.reshape(share, 4))
    turn = [(4 * a + b, 4 * b + a) for a in range(4) for b in range(4)]
    text = lax.ppermute(text_rows, ("y", "z"), turn)
    bias_row = lax.ppermute(proj_bias[None], ("y", "z"), turn)
    *head_parts, affine, swap_half, text, bias_row = after(
        (*head_parts, affine, swap(out_half), text, bias_row)
    )
    residual, stats = call(
        out_body,
        (
            jax.ShapeDtypeStruct((4, MROWS, share), F32),
            jax.ShapeDtypeStruct((MROWS, HD), F32),
        ),
        6,
        scratch=[
            pltpu.VMEM((4, 4 * HD, WINDOW), BF),
            pltpu.VMEM((ROWS, WINDOW), BF),
            pltpu.SemaphoreType.DMA((3,)),
        ],
        in_specs=[SMEM] + [VMEM] * 4 + [ANY] * 3 + [VMEM],
    )(coords, *head_parts, out_half, swap_half, patches, layer_scale[None])
    merged = call(
        merge_body, jax.ShapeDtypeStruct((MROWS, width), BF), 1, in_specs=[VMEM] * 6
    )(*over_z(stats), residual, affine)

    merged_parts = ring(merged, "x")
    merged, image_slots = after((merged, image_slots))
    slots = image_slots.reshape(16, 2, MROWS).transpose(1, 0, 2).reshape(1, 32 * MROWS)
    bias_row = jnp.concatenate([bias_row, bias_row], axis=1)
    merged_parts += [swap(part) for part in merged_parts]
    *merged_parts, slots, bias_row = after((*merged_parts, slots, bias_row))
    summed, *partial = call(
        projection_body,
        [jax.ShapeDtypeStruct((ROWS, ROWS), kind) for kind in (F32, BF, BF, BF)],
        8,
        scratch=[pltpu.VMEM((2 * ROWS, width), BF), pltpu.VMEM((2 * ROWS, width), BF)],
        in_specs=[SMEM] + [VMEM] * 17,
    )(coords, *merged_parts, *proj_parts)
    for k in (1, 2, 3):
        summed = summed + shift(partial[k - 1], "z", k).astype(F32)

    rows = jax.nn.gelu(summed + bias_row, approximate=False).astype(BF)

    row_parts = [rows] + [shift(rows, "y", k) for k in (1, 2, 3)]
    placed, for_sibling = call(
        place_body,
        (
            jax.ShapeDtypeStruct((448, 192), BF),
            jax.ShapeDtypeStruct((448, 192), BF),
        ),
        4,
        scratch=[pltpu.VMEM((8 * ROWS, 192), BF), pltpu.VMEM((2, 448, 192), BF)],
        in_specs=[SMEM] + [VMEM] * 7,
    )(coords, *row_parts, slots, text, text_slots[None])
    placed = jnp.concatenate([placed, swap(for_sibling)], axis=1).reshape(4, 112, ROWS)
    blocks = [placed[0]] + [shift(placed[k], "x", k) for k in (1, 2, 3)]
    stream, squares = call(
        stream_body,
        (
            jax.ShapeDtypeStruct((112, 4 * ROWS), BF),
            jax.ShapeDtypeStruct((112, HD), F32),
        ),
        2,
        in_specs=[SMEM] + [VMEM] * 4,
    )(coords, *blocks)
    squares = over_z(squares)
    squares = ((squares[0] + squares[2]) + (squares[1] + squares[3]))[:, 0:1]
    inverse_rms = lax.rsqrt(squares * (1.0 / 6144) + 1e-05)
    normed = (stream.astype(F32) * inverse_rms * stream_gain).astype(BF)
    return (stream, normed)


def solution(mesh):
    grid = Mesh(mesh.devices.reshape(4, 4, 2, 4), ("y", "x", "c", "z"))
    seq = ("y", "x", "c")
    return jax.shard_map(
        per_device,
        mesh=grid,
        in_specs=(
            P(seq, None),
            P(),
            P(None, "z"),
            P(None, "z"),
            P(None, "z"),
            P("z", None),
            P(),
            P("z"),
            P("z"),
            P("z", seq),
            P(seq),
            P(None, seq),
            P("z"),
            P(),
            P(),
            P(),
        ),
        out_specs=(P(seq, "z"), P(seq, "z")),
        check_vma=False,
    )
```

profile of v0, /device:TPU:0, one launch (start us, length us, event | category | flops | bytes accessed | tf_op | source)
XLA Modules:
  0.0 272.1 jit_solution(17381645819291913303)
XLA Ops:
  1.3 11.8 %shard_map.167 = (bf16[384,384]{1,0:T(8,128)(2,1)}, bf16[384,384]{1,0:T(8,128)(2,1)}, bf16[384,384]{1,0:T(8,128)(2,1)}, bf16[384,384]{1,0:T(8,128)(2,1)}) custom-call(s32[4]{0:T(128)} %pad_add_fusion.s_ref.refs_0_, bf16[384,3200]{1,0:T(8,128)(2,1)} %x_any.1, f32[25,128]{1,0:T(8,128)} %bitcast.20, bf16[3200,512]{1,0:T(8,128)(2,1)} %wk_ref.1, ...), custom_call_target="tpu_custom_call" | custom-call | flops 11000000512 | tf_op jit(solution)/shard_map/pallas_call | solution.py:86
  19.0 4.4 %collective-permute-done.m1 = bf16[384,384]{1,0:T(8,128)(2,1)S(1)} collective-permute-done((bf16[384,384]{1,0:T(8,128)(2,1)}, bf16[384,384]{1,0:T(8,128)(2,1)S(1)}, u32[]{:S(2)}, u32[]{:S(2)}) %collective-permute-start) | collective-permute-done | bytes 294944 | tf_op jit(solution)/shard_map/ppermute | solution.py:21
  23.4 7.5 %collective-permute-done.1.m2 = bf16[384,384]{1,0:T(8,128)(2,1)S(1)} collective-permute-done((bf16[384,384]{1,0:T(8,128)(2,1)}, bf16[384,384]{1,0:T(8,128)(2,1)S(1)}, u32[]{:S(2)}, u32[]{:S(2)}) %collective-permute-start.1) | collective-permute-done | bytes 294944 | tf_op jit(solution)/shard_map/ppermute | solution.py:21
  40.7 15.3 %shard_map.169 = (f32[4,384,256]{2,1,0:T(8,128)}, f32[4,384,128]{2,1,0:T(8,128)}) custom-call(s32[4]{0:T(128)} %pad_add_fusion.s_ref.refs_0_, s32[3]{0:T(128)} %refs_1_.5, bf16[4,384,128]{2,1,0:T(8,128)(2,1)} %get-tuple-element.100.refs_2_, bf16[4,384,256]{2,1,0:T(8,128)(2,1)} %get-tuple-element.109.refs_3_, bf16[4,384,256]{2,1,0:T(8,128)(2,1)} %copy-done.16), custom_call_target="tpu_custom_call" | custom-call | flops 10000000000 | tf_op jit(solution)/shard_map/pallas_call | solution.py:228
  56.0 3.3 %shard_map.170 = bf16[4,256,896]{2,1,0:T(8,128)(2,1)} custom-call(s32[4]{0:T(128)} %pad_add_fusion.s_ref.refs_0_, bf16[512,3200]{1,0:T(8,128)(2,1)} %w_ref), custom_call_target="tpu_custom_call" | custom-call | flops 100000000 | tf_op jit(solution)/shard_map/pallas_call | solution.py:458
  59.9 5.3 %all-to-all-start = ((bf16[4,256,896]{2,1,0:T(8,128)(2,1)}), bf16[4,256,896]{2,1,0:T(8,128)(2,1)S(1)}, u32[]{:S(2)}, u32[]{:S(2)}) async-start(bf16[4,256,896]{2,1,0:T(8,128)(2,1)} %shard_map.170), calls=%async_computation | async-start | bytes 3670016 | tf_op jit(solution)/shard_map/all_to_all | solution.py:468
  68.5 18.4 %shard_map.171 = (f32[4,384,256]{2,1,0:T(8,128)}, f32[4,384,128]{2,1,0:T(8,128)}) custom-call(s32[4]{0:T(128)} %pad_add_fusion.s_ref.refs_0_, s32[3]{0:T(128)} %refs_1_.5, bf16[4,384,128]{2,1,0:T(8,128)(2,1)} %get-tuple-element.100.refs_2_, bf16[4,384,256]{2,1,0:T(8,128)(2,1)} %collective-permute-done.3.refs_3_, ...), custom_call_target="tpu_custom_call" | custom-call | flops 20000000000 | tf_op jit(solution)/shard_map/pallas_call | solution.py:228
  93.5 9.5 %shard_map.172 = (bf16[384,128]{1,0:T(8,128)(2,1)}, bf16[384,128]{1,0:T(8,128)(2,1)}, bf16[384,128]{1,0:T(8,128)(2,1)}, bf16[384,128]{1,0:T(8,128)(2,1)}) custom-call(s32[4]{0:T(128)} %pad_add_fusion.s_ref.refs_0_, s32[3]{0:T(128)} %refs_1_.5, bf16[4,384,128]{2,1,0:T(8,128)(2,1)} %get-tuple-element.100.refs_2_, ...), custom_call_target="tpu_custom_call" | custom-call | flops 10000000000 | tf_op jit(solution)/shard_map/pallas_call | solution.py:221
  105.8 4.9 %collective-permute-done.14 = bf16[384,128]{1,0:T(8,128)(2,1)S(1)} collective-permute-done((bf16[384,128]{1,0:T(8,128)(2,1)}, bf16[384,128]{1,0:T(8,128)(2,1)S(1)}, u32[]{:S(2)}, u32[]{:S(2)}) %collective-permute-start.14) | collective-permute-done | bytes 98336 | tf_op jit(solution)/shard_map/ppermute | solution.py:21
  125.0 9.6 %collective-permute-done.21.o3 = bf16[4,384,128]{2,1,0:T(8,128)(2,1)S(1)} collective-permute-done((bf16[4,384,128]{2,1,0:T(8,128)(2,1)S(1)}, bf16[4,384,128]{2,1,0:T(8,128)(2,1)S(1)}, u32[]{:S(2)}, u32[]{:S(2)}) %collective-permute-start.21) | collective-permute-done | bytes 393248 | tf_op jit(solution)/shard_map/ppermute | solution.py:21
  134.6 10.8 %collective-permute-done.19.o1 = bf16[4,384,128]{2,1,0:T(8,128)(2,1)} collective-permute-done((bf16[4,384,128]{2,1,0:T(8,128)(2,1)S(1)}, bf16[4,384,128]{2,1,0:T(8,128)(2,1)}, u32[]{:S(2)}, u32[]{:S(2)}) %collective-permute-start.19) | collective-permute-done | bytes 393248 | tf_op jit(solution)/shard_map/ppermute | solution.py:21
  145.5 7.3 %shard_map.174 = (f32[4,96,800]{2,1,0:T(8,128)}, f32[96,128]{1,0:T(8,128)}) custom-call(s32[4]{0:T(128)} %pad_add_fusion.s_ref.refs_0_, bf16[4,384,128]{2,1,0:T(8,128)(2,1)} %copy-done.6, bf16[4,384,128]{2,1,0:T(8,128)(2,1)} %collective-permute-done.19.o1, bf16[4,384,128]{2,1,0:T(8,128)(2,1)} %copy-done.22, bf16[4,384,128]{2,1,0:T(8,128)(2,1)} %copy-done.21, ...), custom_call_target="tpu_custom_call" | custom-call | flops 6000000000 | tf_op jit(solution)/shard_map/pallas_call | solution.py:500
  157.7 3.1 %collective-permute-done.26.s2 = f32[96,128]{1,0:T(8,128)S(1)} collective-permute-done((f32[96,128]{1,0:T(8,128)}, f32[96,128]{1,0:T(8,128)S(1)}, u32[]{:S(2)}, u32[]{:S(2)}) %collective-permute-start.26) | collective-permute-done | bytes 49184 | tf_op jit(solution)/shard_map/ppermute | solution.py:21
  163.6 3.1 %shard_map.175.refs_0_ = bf16[96,3200]{1,0:T(8,128)(2,1)} custom-call(f32[96,128]{1,0:T(8,128)} %get-tuple-element.145.s0, f32[96,128]{1,0:T(8,128)} %copy-done.34, f32[96,128]{1,0:T(8,128)} %copy-done.33, f32[96,128]{1,0:T(8,128)} %copy-done.32, f32[4,96,800]{2,1,0:T(8,128)} %get-tuple-element.146.r_ref, f32[8,800]{1,0:T(8,128)} %shard_map.173.affine_ref), custom_call_target="tpu_custom_call" | custom-call | flops 1000000000 | tf_op jit(solution)/shard_map/pallas_call | solution.py:514
  168.8 12.1 %collective-permute-done.30.refs_4_ = bf16[96,3200]{1,0:T(8,128)(2,1)S(1)} collective-permute-done((bf16[96,3200]{1,0:T(8,128)(2,1)}, bf16[96,3200]{1,0:T(8,128)(2,1)S(1)}, u32[]{:S(2)}, u32[]{:S(2)}) %collective-permute-start.30) | collective-permute-done | bytes 614432 | tf_op jit(solution)/shard_map/ppermute | solution.py:21
  183.6 4.3 %collective-permute-done.31.refs_3_ = bf16[48,3200]{1,0:T(8,128)(2,1)} collective-permute-done((bf16[48,3200]{1,0:T(8,128)(2,1)S(1)}, bf16[48,3200]{1,0:T(8,128)(2,1)}, u32[]{:S(2)}, u32[]{:S(2)}) %collective-permute-start.31) | collective-permute-done | bytes 307232 | tf_op jit(solution)/shard_map/ppermute | solution.py:21
  193.5 9.8 %shard_map.176 = (f32[384,384]{1,0:T(8,128)}, bf16[384,384]{1,0:T(8,128)(2,1)}, bf16[384,384]{1,0:T(8,128)(2,1)}, bf16[384,384]{1,0:T(8,128)(2,1)}) custom-call(s32[4]{0:T(128)} %pad_add_fusion.s_ref.refs_0_, bf16[96,3200]{1,0:T(8,128)(2,1)} %shard_map.175.refs_0_, bf16[96,3200]{1,0:T(8,128)(2,1)} %copy-done.10, ...), custom_call_target="tpu_custom_call" | custom-call | flops 8000000000 | tf_op jit(solution)/shard_map/pallas_call | solution.py:524
  206.5 13.9 %collective-permute-done.37 = bf16[384,384]{1,0:T(8,128)(2,1)S(1)} collective-permute-done((bf16[384,384]{1,0:T(8,128)(2,1)}, bf16[384,384]{1,0:T(8,128)(2,1)S(1)}, u32[]{:S(2)}, u32[]{:S(2)}) %collective-permute-start.37) | collective-permute-done | bytes 294944 | tf_op jit(solution)/shard_map/ppermute | solution.py:21
  226.2 7.3 %collective-permute-done.42.r3 = bf16[384,384]{1,0:T(8,128)(2,1)S(1)} collective-permute-done((bf16[384,384]{1,0:T(8,128)(2,1)S(1)}, bf16[384,384]{1,0:T(8,128)(2,1)S(1)}, u32[]{:S(2)}, u32[]{:S(2)}) %collective-permute-start.42) | collective-permute-done | bytes 294944 | tf_op jit(solution)/shard_map/ppermute | solution.py:21
  233.5 3.2 %collective-permute-done.41.r2 = bf16[384,384]{1,0:T(8,128)(2,1)S(1)} collective-permute-done((bf16[384,384]{1,0:T(8,128)(2,1)S(1)}, bf16[384,384]{1,0:T(8,128)(2,1)S(1)}, u32[]{:S(2)}, u32[]{:S(2)}) %collective-permute-start.41) | collective-permute-done | bytes 294944 | tf_op jit(solution)/shard_map/ppermute | solution.py:21
  236.7 4.1 %collective-permute-done.40.r1 = bf16[384,384]{1,0:T(8,128)(2,1)S(1)} collective-permute-done((bf16[384,384]{1,0:T(8,128)(2,1)S(1)}, bf16[384,384]{1,0:T(8,128)(2,1)S(1)}, u32[]{:S(2)}, u32[]{:S(2)}) %collective-permute-start.40) | collective-permute-done | bytes 294944 | tf_op jit(solution)/shard_map/ppermute | solution.py:21
  241.5 4.6 %shard_map.177 = (bf16[448,192]{1,0:T(8,128)(2,1)}, bf16[448,192]{1,0:T(8,128)(2,1)}) custom-call(s32[4]{0:T(128)} %pad_add_fusion.s_ref.refs_0_, bf16[384,384]{1,0:T(8,128)(2,1)} %copy-done.7, bf16[384,384]{1,0:T(8,128)(2,1)} %copy-done.28, bf16[384,384]{1,0:T(8,128)(2,1)} %copy-done.26, bf16[384,384]{1,0:T(8,128)(2,1)} %copy-done.24, ...), custom_call_target="tpu_custom_call" | custom-call | flops 4000000000 | tf_op jit(solution)/shard_map/pallas_call | solution.py:537
  260.2 2.9 %collective-permute-start.49 = (f32[112,128]{1,0:T(8,128)}, f32[112,128]{1,0:T(8,128)S(1)}, u32[]{:S(2)}, u32[]{:S(2)}) collective-permute-start(f32[112,128]{1,0:T(8,128)} %get-tuple-element.177), channel_id=1, source_target_pairs={{0,3},{1,0},{2,1},{3,2},{4,7},{5,4},{6,5},{7,6},{8,11},{9,8},{10,9... | collective-permute-start | bytes 172040 | tf_op jit(solution)/shard_map/ppermute | solution.py:21
  265.2 4.1 %collective-permute-done.48 = f32[112,128]{1,0:T(8,128)S(1)} collective-permute-done((f32[112,128]{1,0:T(8,128)}, f32[112,128]{1,0:T(8,128)S(1)}, u32[]{:S(2)}, u32[]{:S(2)}) %collective-permute-start.48) | collective-permute-done | bytes 57376 | tf_op jit(solution)/shard_map/ppermute | solution.py:21
  (180 shorter events, 90.7 us)
Async XLA Ops:
  14.8 16.2 %collective-permute-start.1 = (bf16[384,384]{1,0:T(8,128)(2,1)}, bf16[384,384]{1,0:T(8,128)(2,1)S(1)}, u32[]{:S(2)}, u32[]{:S(2)}) collective-permute-start(bf16[384,384]{1,0:T(8,128)(2,1)} %get-tuple-element.96), channel_id=1, source_target_pairs={{0,64},{32,96},{64,0},{96,32},{1,65},{33,97},{65,1},{97,33},{2,66}... | collective-permute-start | bytes 884744 | tf_op jit(solution)/shard_map/ppermute | solution.py:21
  17.7 13.3 %collective-permute-start.2 = (bf16[384,384]{1,0:T(8,128)(2,1)}, bf16[384,384]{1,0:T(8,128)(2,1)S(1)}, u32[]{:S(2)}, u32[]{:S(2)}) collective-permute-start(bf16[384,384]{1,0:T(8,128)(2,1)} %get-tuple-element.97), channel_id=1, source_target_pairs={{0,96},{32,0},{64,32},{96,64},{1,97},{33,1},{65,33},{97,65},{2,98}... | collective-permute-start | bytes 884744 | tf_op jit(solution)/shard_map/ppermute | solution.py:21
  34.7 24.6 %collective-permute-start.4 = (bf16[4,384,256]{2,1,0:T(8,128)(2,1)}, bf16[4,384,256]{2,1,0:T(8,128)(2,1)}, u32[]{:S(2)}, u32[]{:S(2)}) collective-permute-start(bf16[4,384,256]{2,1,0:T(8,128)(2,1)} %get-tuple-element.109.refs_3_), channel_id=1, source_target_pairs={{0,24},{8,0},{16,8},{24,16},{1,25},{9,1},{17,9},{25,17},{2,26},{10... | collective-permute-start | bytes 2359304 | tf_op jit(solution)/shard_map/ppermute | solution.py:21
  37.5 21.8 %collective-permute-start.3 = (bf16[4,384,256]{2,1,0:T(8,128)(2,1)}, bf16[4,384,256]{2,1,0:T(8,128)(2,1)}, u32[]{:S(2)}, u32[]{:S(2)}) collective-permute-start(bf16[4,384,256]{2,1,0:T(8,128)(2,1)} %get-tuple-element.109.refs_3_), channel_id=1, source_target_pairs={{0,8},{8,16},{16,24},{24,0},{1,9},{9,17},{17,25},{25,1},{2,10},{10... | collective-permute-start | bytes 2359304 | tf_op jit(solution)/shard_map/ppermute | solution.py:21
  37.6 21.7 %collective-permute-start.7 = (bf16[96,3200]{1,0:T(8,128)(2,1)S(1)}, bf16[96,3200]{1,0:T(8,128)(2,1)}, u32[]{:S(2)}, u32[]{:S(2)}) collective-permute-start(bf16[96,3200]{1,0:T(8,128)(2,1)S(1)} %get-tuple-element.119), channel_id=1, source_target_pairs={{0,96},{32,0},{64,32},{96,64},{1,97},{33,1},{65,33},{97,65},{2,98}... | collective-permute-start | bytes 1843208 | tf_op jit(solution)/shard_map/ppermute | solution.py:21
  39.1 20.2 %collective-permute-start.6 = (bf16[96,3200]{1,0:T(8,128)(2,1)S(1)}, bf16[96,3200]{1,0:T(8,128)(2,1)}, u32[]{:S(2)}, u32[]{:S(2)}) collective-permute-start(bf16[96,3200]{1,0:T(8,128)(2,1)S(1)} %get-tuple-element.120), channel_id=1, source_target_pairs={{0,32},{32,64},{64,96},{96,0},{1,33},{33,65},{65,97},{97,1},{2,34}... | collective-permute-start | bytes 1843208 | tf_op jit(solution)/shard_map/ppermute | solution.py:21
  59.9 29.1 %all-to-all-start = ((bf16[4,256,896]{2,1,0:T(8,128)(2,1)}), bf16[4,256,896]{2,1,0:T(8,128)(2,1)S(1)}, u32[]{:S(2)}, u32[]{:S(2)}) async-start(bf16[4,256,896]{2,1,0:T(8,128)(2,1)} %shard_map.170), calls=%async_computation | async-start | bytes 3670016 | tf_op jit(solution)/shard_map/all_to_all | solution.py:468
  65.2 21.6 %collective-permute-start.11 = (bf16[96,3200]{1,0:T(8,128)(2,1)S(1)}, bf16[96,3200]{1,0:T(8,128)(2,1)}, u32[]{:S(2)}, u32[]{:S(2)}) collective-permute-start(bf16[96,3200]{1,0:T(8,128)(2,1)S(1)} %copy-done.5), channel_id=1, source_target_pairs={{0,32},{32,64},{64,96},{96,0},{1,33},{33,65},{65,97},{97,1},{2,34}... | collective-permute-start | bytes 1843208 | tf_op jit(solution)/shard_map/ppermute | solution.py:21
  65.8 21.1 %collective-permute-start.12 = (bf16[96,3200]{1,0:T(8,128)(2,1)S(1)}, bf16[96,3200]{1,0:T(8,128)(2,1)}, u32[]{:S(2)}, u32[]{:S(2)}) collective-permute-start(bf16[96,3200]{1,0:T(8,128)(2,1)S(1)} %copy-done.3), channel_id=1, source_target_pairs={{0,96},{32,0},{64,32},{96,64},{1,97},{33,1},{65,33},{97,65},{2,98}... | collective-permute-start | bytes 1843208 | tf_op jit(solution)/shard_map/ppermute | solution.py:21
  68.5 20.5 %collective-permute-start.8 = (bf16[4,384,256]{2,1,0:T(8,128)(2,1)}, bf16[4,384,256]{2,1,0:T(8,128)(2,1)}, u32[]{:S(2)}, u32[]{:S(2)}) collective-permute-start(bf16[4,384,256]{2,1,0:T(8,128)(2,1)} %get-tuple-element.109.refs_3_), channel_id=1, source_target_pairs={{0,16},{8,24},{16,0},{24,8},{1,17},{9,25},{17,1},{25,9},{2,18},{10... | collective-permute-start | bytes 2359304 | tf_op jit(solution)/shard_map/ppermute | solution.py:21
  89.3 24.6 %collective-permute-start.17 = (bf16[96,3200]{1,0:T(8,128)(2,1)}, bf16[96,3200]{1,0:T(8,128)(2,1)}, u32[]{:S(2)}, u32[]{:S(2)}) collective-permute-start(bf16[96,3200]{1,0:T(8,128)(2,1)} %collective-permute-done.6.refs_11_), channel_id=1, source_target_pairs={{0,32},{32,64},{64,96},{96,0},{1,33},{33,65},{65,97},{97,1},{2,34}... | collective-permute-start | bytes 1843208 | tf_op jit(solution)/shard_map/ppermute | solution.py:21
  89.9 24.0 %collective-permute-start.18 = (bf16[96,3200]{1,0:T(8,128)(2,1)}, bf16[96,3200]{1,0:T(8,128)(2,1)}, u32[]{:S(2)}, u32[]{:S(2)}) collective-permute-start(bf16[96,3200]{1,0:T(8,128)(2,1)} %collective-permute-done.7.refs_16_), channel_id=1, source_target_pairs={{0,96},{32,0},{64,32},{96,64},{1,97},{33,1},{65,33},{97,65},{2,98}... | collective-permute-start | bytes 1843208 | tf_op jit(solution)/shard_map/ppermute | solution.py:21
  113.9 31.5 %collective-permute-start.22 = (bf16[4,256,896]{2,1,0:T(8,128)(2,1)S(1)}, bf16[4,256,896]{2,1,0:T(8,128)(2,1)}, u32[]{:S(2)}, u32[]{:S(2)}) collective-permute-start(bf16[4,256,896]{2,1,0:T(8,128)(2,1)S(1)} %all-to-all-done.mine), channel_id=1, source_target_pairs={{0,4},{4,0},{1,5},{5,1},{2,6},{6,2},{3,7},{7,3},{8,12},{12,8},{9,1... | collective-permute-start | bytes 5505032 | tf_op jit(solution)/shard_map/ppermute | solution.py:25
  114.0 20.6 %collective-permute-start.21 = (bf16[4,384,128]{2,1,0:T(8,128)(2,1)S(1)}, bf16[4,384,128]{2,1,0:T(8,128)(2,1)S(1)}, u32[]{:S(2)}, u32[]{:S(2)}) collective-permute-start(bf16[4,384,128]{2,1,0:T(8,128)(2,1)S(1)} %pad_maximum_fusion.o0), channel_id=1, source_target_pairs={{0,3},{1,0},{2,1},{3,2},{4,7},{5,4},{6,5},{7,6},{8,11},{9,8},{10,9... | collective-permute-start | bytes 1179656 | tf_op jit(solution)/shard_map/ppermute | solution.py:21
  116.1 18.5 %collective-permute-start.20 = (bf16[4,384,128]{2,1,0:T(8,128)(2,1)S(1)}, bf16[4,384,128]{2,1,0:T(8,128)(2,1)S(1)}, u32[]{:S(2)}, u32[]{:S(2)}) collective-permute-start(bf16[4,384,128]{2,1,0:T(8,128)(2,1)S(1)} %pad_maximum_fusion.o0), channel_id=1, source_target_pairs={{0,2},{1,3},{2,0},{3,1},{4,6},{5,7},{6,4},{7,5},{8,10},{9,11},{10,... | collective-permute-start | bytes 1179656 | tf_op jit(solution)/shard_map/ppermute | solution.py:21
  117.0 28.4 %collective-permute-start.19 = (bf16[4,384,128]{2,1,0:T(8,128)(2,1)S(1)}, bf16[4,384,128]{2,1,0:T(8,128)(2,1)}, u32[]{:S(2)}, u32[]{:S(2)}) collective-permute-start(bf16[4,384,128]{2,1,0:T(8,128)(2,1)S(1)} %pad_maximum_fusion.o0), channel_id=1, source_target_pairs={{0,1},{1,2},{2,3},{3,0},{4,5},{5,6},{6,7},{7,4},{8,9},{9,10},{10,1... | collective-permute-start | bytes 1179656 | tf_op jit(solution)/shard_map/ppermute | solution.py:21
  166.8 14.1 %collective-permute-start.30 = (bf16[96,3200]{1,0:T(8,128)(2,1)}, bf16[96,3200]{1,0:T(8,128)(2,1)S(1)}, u32[]{:S(2)}, u32[]{:S(2)}) collective-permute-start(bf16[96,3200]{1,0:T(8,128)(2,1)} %shard_map.175.refs_0_), channel_id=1, source_target_pairs={{0,24},{8,0},{16,8},{24,16},{1,25},{9,1},{17,9},{25,17},{2,26},{10... | collective-permute-start | bytes 1843208 | tf_op jit(solution)/shard_map/ppermute | solution.py:21
  166.9 15.5 %collective-permute-start.28 = (bf16[96,3200]{1,0:T(8,128)(2,1)}, bf16[96,3200]{1,0:T(8,128)(2,1)S(1)}, u32[]{:S(2)}, u32[]{:S(2)}) collective-permute-start(bf16[96,3200]{1,0:T(8,128)(2,1)} %shard_map.175.refs_0_), channel_id=1, source_target_pairs={{0,8},{8,16},{16,24},{24,0},{1,9},{9,17},{17,25},{25,1},{2,10},{10... | collective-permute-start | bytes 1843208 | tf_op jit(solution)/shard_map/ppermute | solution.py:21
  168.8 22.7 %collective-permute-start.32 = (bf16[96,3200]{1,0:T(8,128)(2,1)}, bf16[96,3200]{1,0:T(8,128)(2,1)S(1)}, u32[]{:S(2)}, u32[]{:S(2)}) collective-permute-start(bf16[96,3200]{1,0:T(8,128)(2,1)} %shard_map.175.refs_0_), channel_id=1, source_target_pairs={{0,4},{4,0},{1,5},{5,1},{2,6},{6,2},{3,7},{7,3},{8,12},{12,8},{9,1... | collective-permute-start | bytes 1843208 | tf_op jit(solution)/shard_map/ppermute | solution.py:25
  203.3 17.1 %collective-permute-start.37 = (bf16[384,384]{1,0:T(8,128)(2,1)}, bf16[384,384]{1,0:T(8,128)(2,1)S(1)}, u32[]{:S(2)}, u32[]{:S(2)}) collective-permute-start(bf16[384,384]{1,0:T(8,128)(2,1)} %get-tuple-element.168), channel_id=1, source_target_pairs={{0,1},{1,2},{2,3},{3,0},{4,5},{5,6},{6,7},{7,4},{8,9},{9,10},{10,1... | collective-permute-start | bytes 884744 | tf_op jit(solution)/shard_map/ppermute | solution.py:21
  203.3 17.1 %collective-permute-start.38 = (bf16[384,384]{1,0:T(8,128)(2,1)}, bf16[384,384]{1,0:T(8,128)(2,1)S(1)}, u32[]{:S(2)}, u32[]{:S(2)}) collective-permute-start(bf16[384,384]{1,0:T(8,128)(2,1)} %get-tuple-element.169), channel_id=1, source_target_pairs={{0,2},{1,3},{2,0},{3,1},{4,6},{5,7},{6,4},{7,5},{8,10},{9,11},{10,... | collective-permute-start | bytes 884744 | tf_op jit(solution)/shard_map/ppermute | solution.py:21
  204.7 16.3 %collective-permute-start.39 = (bf16[384,384]{1,0:T(8,128)(2,1)}, bf16[384,384]{1,0:T(8,128)(2,1)S(1)}, u32[]{:S(2)}, u32[]{:S(2)}) collective-permute-start(bf16[384,384]{1,0:T(8,128)(2,1)} %get-tuple-element.170), channel_id=1, source_target_pairs={{0,3},{1,0},{2,1},{3,2},{4,7},{5,4},{6,5},{7,6},{8,11},{9,8},{10,9... | collective-permute-start | bytes 884744 | tf_op jit(solution)/shard_map/ppermute | solution.py:21
  225.3 11.4 %collective-permute-start.41 = (bf16[384,384]{1,0:T(8,128)(2,1)S(1)}, bf16[384,384]{1,0:T(8,128)(2,1)S(1)}, u32[]{:S(2)}, u32[]{:S(2)}) collective-permute-start(bf16[384,384]{1,0:T(8,128)(2,1)S(1)} %fusion.2.r0), channel_id=1, source_target_pairs={{0,64},{32,96},{64,0},{96,32},{1,65},{33,97},{65,1},{97,33},{2,66}... | collective-permute-start | bytes 884744 | tf_op jit(solution)/shard_map/ppermute | solution.py:21
  225.3 15.5 %collective-permute-start.40 = (bf16[384,384]{1,0:T(8,128)(2,1)S(1)}, bf16[384,384]{1,0:T(8,128)(2,1)S(1)}, u32[]{:S(2)}, u32[]{:S(2)}) collective-permute-start(bf16[384,384]{1,0:T(8,128)(2,1)S(1)} %fusion.2.r0), channel_id=1, source_target_pairs={{0,32},{32,64},{64,96},{96,0},{1,33},{33,65},{65,97},{97,1},{2,34}... | collective-permute-start | bytes 884744 | tf_op jit(solution)/shard_map/ppermute | solution.py:21
  (63 other events, 571.8 us)
where the time goes:
time: 274 us; the launch traced here: 272 us
  waiting for transfers between devices  109 us (40%)
  Pallas kernels  89.5 us (33%)
  starting transfers between devices  54.3 us (20%)
  local copies, waits for them, and re-layouts  10.2 us (4%)
  other arithmetic  8.63 us (3%)
    ppermute x37, waiting for transfers between devices, shift(): return lax.ppermute(value, axis, [(i, (i + k) % 4) for i in range(4)])  106 us
    ppermute x37, starting transfers between devices, shift(): return lax.ppermute(value, axis, [(i, (i + k) % 4) for i in range(4)])  45.5 us
    pallas_call x2, Pallas kernels, attend(): call(body, state_shapes, 2.5 * len(steps), scratch=held, in_specs=specs)  33.7 us
    pallas_call x1, Pallas kernels, project_qkv(): pl.pallas_call(qkv_body, out_shape=[jax.ShapeDtypeStruct((ROWS, 3 * HD),...  11.8 us
    pallas_call x1, Pallas kernels, per_device(): call(projection_body, [jax.ShapeDtypeStruct((ROWS, ROWS), kind) for kind...  9.81 us
    pallas_call x1, Pallas kernels, attend(): call(body, [jax.ShapeDtypeStruct((ROWS, HD), BF)] * 4, 2.5 * len(steps),...  9.46 us
    pallas_call x1, Pallas kernels, per_device(): call(out_body, (jax.ShapeDtypeStruct((4, MROWS, share), F32), jax.ShapeDt...  7.3 us
    unnamed x72, local copies, waits for them, and re-layouts  6.16 us
  transfers between devices with their start and end apart: 51, of which 26 were waited for; matrix products, arithmetic and copies ran while one was open for 2% of the time, Pallas kernels for 18%

commit v1 on v0

--- a/solution.py
+++ b/solution.py
@@ -437,6 +437,13 @@
 
     kvq, out_weight = after((kvq, out_weight))
     moved = [kvq[0]] + [shift(kvq[k], "y", k) for k in (1, 2, 3)]
+    windows = call(
+        window_body,
+        jax.ShapeDtypeStruct((4, out_weight.shape[0] // 2, WINDOW), BF),
+        0.1,
+        in_specs=[SMEM, VMEM],
+    )(coords, out_weight)
+    windows, *moved = after((windows, *moved))
     kv_own, q_own = call(
         pack_body,
         (
@@ -454,13 +461,6 @@
 
     where = (coords, tile_counts, q_own)
     state = attend((0,) * 4, *where, [kv_own, kv_sib], None, False)
-    out_weight, state = after((out_weight, state))
-    windows = call(
-        window_body,
-        jax.ShapeDtypeStruct((4, out_weight.shape[0] // 2, WINDOW), BF),
-        0.1,
-        in_specs=[SMEM, VMEM],
-    )(coords, out_weight)
     near, state, windows, back_low, ahead_high, proj_low, proj_high, kv_here = after(
         (near, state, windows, back_low, ahead_high, proj_low, proj_high, kv_own)
     )
@@ -481,22 +481,17 @@
         ahead_low,
         ahead_high,
     ]
+    swap_half = swap(out_half)
     attended = attend((2,) * 4, *where, [far, swap(far)], state, True)
+    attended, proj_parts, swap_half = after((attended, proj_parts, swap_half))
     heads = jnp.stack([attended[0]] + [shift(attended[k], "y", 4 - k) for k in (1, 2, 3)])
-    heads, merge_gain, merge_bias, layer_scale, text_rows, proj_bias, proj_parts, out_half = after(
-        (heads, merge_gain, merge_bias, layer_scale, text_rows, proj_bias, proj_parts, out_half)
-    )
+    heads, merge_gain, merge_bias, layer_scale = after((heads, merge_gain, merge_bias, layer_scale))
 
     head_parts = [heads] + [shift(heads, "z", k) for k in (1, 2, 3)]
     affine = call(
         turn_body, jax.ShapeDtypeStruct((8, share), F32), 1, in_specs=[VMEM] * 2
     )(merge_gain.reshape(share, 4), merge_bias.reshape(share, 4))
-    turn = [(4 * a + b, 4 * b + a) for a in range(4) for b in range(4)]
-    text = lax.ppermute(text_rows, ("y", "z"), turn)
-    bias_row = lax.ppermute(proj_bias[None], ("y", "z"), turn)
-    *head_parts, affine, swap_half, text, bias_row = after(
-        (*head_parts, affine, swap(out_half), text, bias_row)
-    )
+    *head_parts, affine = after((*head_parts, affine))
     residual, stats = call(
         out_body,
         (
@@ -516,11 +511,14 @@
     )(*over_z(stats), residual, affine)
 
     merged_parts = ring(merged, "x")
-    merged, image_slots = after((merged, image_slots))
+    merged, image_slots, text_rows, proj_bias = after((merged, image_slots, text_rows, proj_bias))
+    turn = [(4 * a + b, 4 * b + a) for a in range(4) for b in range(4)]
+    text = lax.ppermute(text_rows, ("y", "z"), turn)
+    bias_row = lax.ppermute(proj_bias[None], ("y", "z"), turn)
     slots = image_slots.reshape(16, 2, MROWS).transpose(1, 0, 2).reshape(1, 32 * MROWS)
     bias_row = jnp.concatenate([bias_row, bias_row], axis=1)
     merged_parts += [swap(part) for part in merged_parts]
-    *merged_parts, slots, bias_row = after((*merged_parts, slots, bias_row))
+    *merged_parts, slots, text, bias_row = after((*merged_parts, slots, text, bias_row))
     summed, *partial = call(
         projection_body,
         [jax.ShapeDtypeStruct((ROWS, ROWS), kind) for kind in (F32, BF, BF, BF)],

time: 274 us -> 266 us (0.971)
  waiting for transfers between devices: 109 us -> 98.4 us
    ppermute x37, waiting for transfers between devices: 106 us -> 94.7 us  [shift(): return lax.ppermute(value, axis, [(i, (i + k) % 4) for i in range(4)])]
    unnamed x72 -> x84, local copies, waits for them, and re-layouts: 6.16 us -> 6.82 us
  transfers between devices with their start and end apart: 51 -> 51, of which waited for: 26 -> 31; matrix products, arithmetic and copies ran while one was open for 2% -> 2% of each run, Pallas kernels for 18% -> 18%
where the time goes in v1:
time: 266 us; the launch traced here: 265 us
  waiting for transfers between devices  98.4 us (37%)
  Pallas kernels  89.5 us (34%)
  starting transfers between devices  56.5 us (21%)
  local copies, waits for them, and re-layouts  10.8 us (4%)
  other arithmetic  8.63 us (3%)
    ppermute x37, waiting for transfers between devices, shift(): return lax.ppermute(value, axis, [(i, (i + k) % 4) for i in range(4)])  94.7 us
    ppermute x37, starting transfers between devices, shift(): return lax.ppermute(value, axis, [(i, (i + k) % 4) for i in range(4)])  47.9 us
    pallas_call x2, Pallas kernels, attend(): call(body, state_shapes, 2.5 * len(steps), scratch=held, in_specs=specs)  33.7 us
    pallas_call x1, Pallas kernels, project_qkv(): pl.pallas_call(qkv_body, out_shape=[jax.ShapeDtypeStruct((ROWS, 3 * HD),...  11.8 us
    pallas_call x1, Pallas kernels, per_device(): call(projection_body, [jax.ShapeDtypeStruct((ROWS, ROWS), kind) for kind...  9.78 us
    pallas_call x1, Pallas kernels, attend(): call(body, [jax.ShapeDtypeStruct((ROWS, HD), BF)] * 4, 2.5 * len(steps),...  9.44 us
    pallas_call x1, Pallas kernels, per_device(): call(out_body, (jax.ShapeDtypeStruct((4, MROWS, share), F32), jax.ShapeDt...  7.29 us
    unnamed x84, local copies, waits for them, and re-layouts  6.82 us
  transfers between devices with their start and end apart: 51, of which 31 were waited for; matrix products, arithmetic and copies ran while one was open for 2% of the time, Pallas kernels for 18%

profile of v1, /device:TPU:0, one launch (start us, length us, event | category | flops | bytes accessed | tf_op | source)
XLA Modules:
  0.0 264.8 jit_solution(12683708023257157367)
XLA Ops:
  1.3 11.8 %shard_map.167 = (bf16[384,384]{1,0:T(8,128)(2,1)}, bf16[384,384]{1,0:T(8,128)(2,1)}, bf16[384,384]{1,0:T(8,128)(2,1)}, bf16[384,384]{1,0:T(8,128)(2,1)}) custom-call(s32[4]{0:T(128)} %pad_add_fusion.s_ref.refs_0_, bf16[384,3200]{1,0:T(8,128)(2,1)} %x_any.1, f32[25,128]{1,0:T(8,128)} %bitcast.20, bf16[3200,512]{1,0:T(8,128)(2,1)} %wk_ref.1, ...), custom_call_target="tpu_custom_call" | custom-call | flops 11000000512 | tf_op jit(solution)/shard_map/pallas_call | solution.py:86
  19.0 3.3 %shard_map.168 = bf16[4,256,896]{2,1,0:T(8,128)(2,1)} custom-call(s32[4]{0:T(128)} %pad_add_fusion.s_ref.refs_0_, bf16[512,3200]{1,0:T(8,128)(2,1)} %w_ref), custom_call_target="tpu_custom_call" | custom-call | flops 100000000 | tf_op jit(solution)/shard_map/pallas_call | solution.py:440
  23.4 7.5 %collective-permute-done.1.m2 = bf16[384,384]{1,0:T(8,128)(2,1)S(1)} collective-permute-done((bf16[384,384]{1,0:T(8,128)(2,1)}, bf16[384,384]{1,0:T(8,128)(2,1)S(1)}, u32[]{:S(2)}, u32[]{:S(2)}) %collective-permute-start.1) | collective-permute-done | bytes 294944 | tf_op jit(solution)/shard_map/ppermute | solution.py:21
  39.7 15.3 %shard_map.170 = (f32[4,384,256]{2,1,0:T(8,128)}, f32[4,384,128]{2,1,0:T(8,128)}) custom-call(s32[4]{0:T(128)} %pad_add_fusion.s_ref.refs_0_, s32[3]{0:T(128)} %refs_1_.5, bf16[4,384,128]{2,1,0:T(8,128)(2,1)} %get-tuple-element.109.refs_2_, bf16[4,384,256]{2,1,0:T(8,128)(2,1)} %get-tuple-element.115.refs_3_, bf16[4,384,256]{2,1,0:T(8,128)(2,1)} %collective-permute-done.5.refs_4_), custom_call_target="tpu_custom_call" | custom-call | flops 10000000000 | tf_op jit(solution)/shard_map/pallas_call | solution.py:228
  60.0 5.3 %all-to-all-start = ((bf16[4,256,896]{2,1,0:T(8,128)(2,1)}), bf16[4,256,896]{2,1,0:T(8,128)(2,1)S(1)}, u32[]{:S(2)}, u32[]{:S(2)}) async-start(bf16[4,256,896]{2,1,0:T(8,128)(2,1)} %shard_map.168), calls=%async_computation | async-start | bytes 3670016 | tf_op jit(solution)/shard_map/all_to_all | solution.py:468
  68.5 18.4 %shard_map.171 = (f32[4,384,256]{2,1,0:T(8,128)}, f32[4,384,128]{2,1,0:T(8,128)}) custom-call(s32[4]{0:T(128)} %pad_add_fusion.s_ref.refs_0_, s32[3]{0:T(128)} %refs_1_.5, bf16[4,384,128]{2,1,0:T(8,128)(2,1)} %get-tuple-element.109.refs_2_, bf16[4,384,256]{2,1,0:T(8,128)(2,1)} %copy-done.17, bf16[4,384,256]{2,1,0:T(8,128)(2,1)} %collective-permute-done.9.refs_4_, ...), custom_call_target="tpu_custom_call" | custom-call | flops 20000000000 | tf_op jit(solution)/shard_map/pallas_call | solution.py:228
  94.9 9.4 %shard_map.172 = (bf16[384,128]{1,0:T(8,128)(2,1)}, bf16[384,128]{1,0:T(8,128)(2,1)}, bf16[384,128]{1,0:T(8,128)(2,1)}, bf16[384,128]{1,0:T(8,128)(2,1)}) custom-call(s32[4]{0:T(128)} %pad_add_fusion.s_ref.refs_0_, s32[3]{0:T(128)} %refs_1_.5, bf16[4,384,128]{2,1,0:T(8,128)(2,1)} %get-tuple-element.109.refs_2_, ...), custom_call_target="tpu_custom_call" | custom-call | flops 10000000000 | tf_op jit(solution)/shard_map/pallas_call | solution.py:221
  107.0 3.1 %collective-permute-start.17 = (bf16[384,128]{1,0:T(8,128)(2,1)}, bf16[384,128]{1,0:T(8,128)(2,1)S(1)}, u32[]{:S(2)}, u32[]{:S(2)}) collective-permute-start(bf16[384,128]{1,0:T(8,128)(2,1)} %get-tuple-element.140), channel_id=1, source_target_pairs={{0,96},{32,0},{64,32},{96,64},{1,97},{33,1},{65,33},{97,65},{2,98}... | collective-permute-start | bytes 294920 | tf_op jit(solution)/shard_map/ppermute | solution.py:21
  118.1 3.0 %collective-permute-start.22 = (bf16[4,384,128]{2,1,0:T(8,128)(2,1)S(1)}, bf16[4,384,128]{2,1,0:T(8,128)(2,1)S(1)}, u32[]{:S(2)}, u32[]{:S(2)}) collective-permute-start(bf16[4,384,128]{2,1,0:T(8,128)(2,1)S(1)} %pad_maximum_fusion.o0), channel_id=1, source_target_pairs={{0,3},{1,0},{2,1},{3,2},{4,7},{5,4},{6,5},{7,6},{8,11},{9,8},{10,9... | collective-permute-start | bytes 1179656 | tf_op jit(solution)/shard_map/ppermute | solution.py:21
  127.9 7.8 %collective-permute-done.22.o3 = bf16[4,384,128]{2,1,0:T(8,128)(2,1)S(1)} collective-permute-done((bf16[4,384,128]{2,1,0:T(8,128)(2,1)S(1)}, bf16[4,384,128]{2,1,0:T(8,128)(2,1)S(1)}, u32[]{:S(2)}, u32[]{:S(2)}) %collective-permute-start.22) | collective-permute-done | bytes 393248 | tf_op jit(solution)/shard_map/ppermute | solution.py:21
  135.6 3.7 %collective-permute-done.20.o1 = bf16[4,384,128]{2,1,0:T(8,128)(2,1)S(1)} collective-permute-done((bf16[4,384,128]{2,1,0:T(8,128)(2,1)S(1)}, bf16[4,384,128]{2,1,0:T(8,128)(2,1)S(1)}, u32[]{:S(2)}, u32[]{:S(2)}) %collective-permute-start.20) | collective-permute-done | bytes 393248 | tf_op jit(solution)/shard_map/ppermute | solution.py:21
  140.1 7.3 %shard_map.174 = (f32[4,96,800]{2,1,0:T(8,128)}, f32[96,128]{1,0:T(8,128)}) custom-call(s32[4]{0:T(128)} %pad_add_fusion.s_ref.refs_0_, bf16[4,384,128]{2,1,0:T(8,128)(2,1)} %copy-done.6, bf16[4,384,128]{2,1,0:T(8,128)(2,1)} %copy-done.27, bf16[4,384,128]{2,1,0:T(8,128)(2,1)} %copy-done.26, bf16[4,384,128]{2,1,0:T(8,128)(2,1)} %copy-done.25, ...), custom_call_target="tpu_custom_call" | custom-call | flops 6000000000 | tf_op jit(solution)/shard_map/pallas_call | solution.py:495
  155.4 3.1 %shard_map.175.refs_0_ = bf16[96,3200]{1,0:T(8,128)(2,1)} custom-call(f32[96,128]{1,0:T(8,128)} %get-tuple-element.152.s0, f32[96,128]{1,0:T(8,128)} %copy-done.40, f32[96,128]{1,0:T(8,128)} %copy-done.39, f32[96,128]{1,0:T(8,128)} %copy-done.38, f32[4,96,800]{2,1,0:T(8,128)} %get-tuple-element.153.r_ref, f32[8,800]{1,0:T(8,128)} %shard_map.173.affine_ref), custom_call_target="tpu_custom_call" | custom-call | flops 1000000000 | tf_op jit(solution)/shard_map/pallas_call | solution.py:509
  162.2 10.6 %collective-permute-done.28.refs_4_ = bf16[96,3200]{1,0:T(8,128)(2,1)S(1)} collective-permute-done((bf16[96,3200]{1,0:T(8,128)(2,1)}, bf16[96,3200]{1,0:T(8,128)(2,1)S(1)}, u32[]{:S(2)}, u32[]{:S(2)}) %collective-permute-start.28) | collective-permute-done | bytes 614432 | tf_op jit(solution)/shard_map/ppermute | solution.py:21
  175.7 4.1 %collective-permute-done.29.refs_3_ = bf16[48,3200]{1,0:T(8,128)(2,1)} collective-permute-done((bf16[48,3200]{1,0:T(8,128)(2,1)S(1)}, bf16[48,3200]{1,0:T(8,128)(2,1)}, u32[]{:S(2)}, u32[]{:S(2)}) %collective-permute-start.29) | collective-permute-done | bytes 307232 | tf_op jit(solution)/shard_map/ppermute | solution.py:21
  179.9 3.4 %collective-permute-done.27.refs_2_ = bf16[48,3200]{1,0:T(8,128)(2,1)} collective-permute-done((bf16[48,3200]{1,0:T(8,128)(2,1)S(1)}, bf16[48,3200]{1,0:T(8,128)(2,1)}, u32[]{:S(2)}, u32[]{:S(2)}) %collective-permute-start.27) | collective-permute-done | bytes 307232 | tf_op jit(solution)/shard_map/ppermute | solution.py:21
  186.1 9.8 %shard_map.176 = (f32[384,384]{1,0:T(8,128)}, bf16[384,384]{1,0:T(8,128)(2,1)}, bf16[384,384]{1,0:T(8,128)(2,1)}, bf16[384,384]{1,0:T(8,128)(2,1)}) custom-call(s32[4]{0:T(128)} %pad_add_fusion.s_ref.refs_0_, bf16[96,3200]{1,0:T(8,128)(2,1)} %shard_map.175.refs_0_, bf16[96,3200]{1,0:T(8,128)(2,1)} %copy-done.10, ...), custom_call_target="tpu_custom_call" | custom-call | flops 8000000000 | tf_op jit(solution)/shard_map/pallas_call | solution.py:522
  200.3 6.5 %collective-permute-done.37 = bf16[384,384]{1,0:T(8,128)(2,1)S(1)} collective-permute-done((bf16[384,384]{1,0:T(8,128)(2,1)}, bf16[384,384]{1,0:T(8,128)(2,1)S(1)}, u32[]{:S(2)}, u32[]{:S(2)}) %collective-permute-start.37) | collective-permute-done | bytes 294944 | tf_op jit(solution)/shard_map/ppermute | solution.py:21
  206.8 6.5 %collective-permute-done.38 = bf16[384,384]{1,0:T(8,128)(2,1)S(1)} collective-permute-done((bf16[384,384]{1,0:T(8,128)(2,1)}, bf16[384,384]{1,0:T(8,128)(2,1)S(1)}, u32[]{:S(2)}, u32[]{:S(2)}) %collective-permute-start.38) | collective-permute-done | bytes 294944 | tf_op jit(solution)/shard_map/ppermute | solution.py:21
  219.9 6.1 %collective-permute-done.42.r3 = bf16[384,384]{1,0:T(8,128)(2,1)S(1)} collective-permute-done((bf16[384,384]{1,0:T(8,128)(2,1)S(1)}, bf16[384,384]{1,0:T(8,128)(2,1)S(1)}, u32[]{:S(2)}, u32[]{:S(2)}) %collective-permute-start.42) | collective-permute-done | bytes 294944 | tf_op jit(solution)/shard_map/ppermute | solution.py:21
  228.8 4.3 %collective-permute-done.40.r1 = bf16[384,384]{1,0:T(8,128)(2,1)S(1)} collective-permute-done((bf16[384,384]{1,0:T(8,128)(2,1)S(1)}, bf16[384,384]{1,0:T(8,128)(2,1)S(1)}, u32[]{:S(2)}, u32[]{:S(2)}) %collective-permute-start.40) | collective-permute-done | bytes 294944 | tf_op jit(solution)/shard_map/ppermute | solution.py:21
  233.9 4.6 %shard_map.177 = (bf16[448,192]{1,0:T(8,128)(2,1)}, bf16[448,192]{1,0:T(8,128)(2,1)}) custom-call(s32[4]{0:T(128)} %pad_add_fusion.s_ref.refs_0_, bf16[384,384]{1,0:T(8,128)(2,1)} %copy-done.7, bf16[384,384]{1,0:T(8,128)(2,1)} %copy-done.33, bf16[384,384]{1,0:T(8,128)(2,1)} %copy-done.31, bf16[384,384]{1,0:T(8,128)(2,1)} %copy-done.29, ...), custom_call_target="tpu_custom_call" | custom-call | flops 4000000000 | tf_op jit(solution)/shard_map/pallas_call | solution.py:535
  252.5 3.3 %collective-permute-start.49 = (f32[112,128]{1,0:T(8,128)}, f32[112,128]{1,0:T(8,128)S(1)}, u32[]{:S(2)}, u32[]{:S(2)}) collective-permute-start(f32[112,128]{1,0:T(8,128)} %get-tuple-element.185), channel_id=1, source_target_pairs={{0,3},{1,0},{2,1},{3,2},{4,7},{5,4},{6,5},{7,6},{8,11},{9,8},{10,9... | collective-permute-start | bytes 172040 | tf_op jit(solution)/shard_map/ppermute | solution.py:21
  258.0 4.1 %collective-permute-done.48 = f32[112,128]{1,0:T(8,128)S(1)} collective-permute-done((f32[112,128]{1,0:T(8,128)}, f32[112,128]{1,0:T(8,128)S(1)}, u32[]{:S(2)}, u32[]{:S(2)}) %collective-permute-start.48) | collective-permute-done | bytes 57376 | tf_op jit(solution)/shard_map/ppermute | solution.py:21
  (192 shorter events, 101.5 us)
Async XLA Ops:
  14.8 16.1 %collective-permute-start.1 = (bf16[384,384]{1,0:T(8,128)(2,1)}, bf16[384,384]{1,0:T(8,128)(2,1)S(1)}, u32[]{:S(2)}, u32[]{:S(2)}) collective-permute-start(bf16[384,384]{1,0:T(8,128)(2,1)} %get-tuple-element.101), channel_id=1, source_target_pairs={{0,64},{32,96},{64,0},{96,32},{1,65},{33,97},{65,1},{97,33},{2,66}... | collective-permute-start | bytes 884744 | tf_op jit(solution)/shard_map/ppermute | solution.py:21
  17.7 13.3 %collective-permute-start.2 = (bf16[384,384]{1,0:T(8,128)(2,1)}, bf16[384,384]{1,0:T(8,128)(2,1)S(1)}, u32[]{:S(2)}, u32[]{:S(2)}) collective-permute-start(bf16[384,384]{1,0:T(8,128)(2,1)} %get-tuple-element.102), channel_id=1, source_target_pairs={{0,96},{32,0},{64,32},{96,64},{1,97},{33,1},{65,33},{97,65},{2,98}... | collective-permute-start | bytes 884744 | tf_op jit(solution)/shard_map/ppermute | solution.py:21
  34.7 21.3 %collective-permute-start.4 = (bf16[4,384,256]{2,1,0:T(8,128)(2,1)}, bf16[4,384,256]{2,1,0:T(8,128)(2,1)S(1)}, u32[]{:S(2)}, u32[]{:S(2)}) collective-permute-start(bf16[4,384,256]{2,1,0:T(8,128)(2,1)} %get-tuple-element.115.refs_3_), channel_id=1, source_target_pairs={{0,24},{8,0},{16,8},{24,16},{1,25},{9,1},{17,9},{25,17},{2,26},{10... | collective-permute-start | bytes 2359304 | tf_op jit(solution)/shard_map/ppermute | solution.py:21
  37.5 21.1 %collective-permute-start.3 = (bf16[4,384,256]{2,1,0:T(8,128)(2,1)}, bf16[4,384,256]{2,1,0:T(8,128)(2,1)S(1)}, u32[]{:S(2)}, u32[]{:S(2)}) collective-permute-start(bf16[4,384,256]{2,1,0:T(8,128)(2,1)} %get-tuple-element.115.refs_3_), channel_id=1, source_target_pairs={{0,8},{8,16},{16,24},{24,0},{1,9},{9,17},{17,25},{25,1},{2,10},{10... | collective-permute-start | bytes 2359304 | tf_op jit(solution)/shard_map/ppermute | solution.py:21
  37.6 17.4 %collective-permute-start.7 = (bf16[96,3200]{1,0:T(8,128)(2,1)S(1)}, bf16[96,3200]{1,0:T(8,128)(2,1)S(1)}, u32[]{:S(2)}, u32[]{:S(2)}) collective-permute-start(bf16[96,3200]{1,0:T(8,128)(2,1)S(1)} %get-tuple-element.125), channel_id=1, source_target_pairs={{0,96},{32,0},{64,32},{96,64},{1,97},{33,1},{65,33},{97,65},{2,98}... | collective-permute-start | bytes 1843208 | tf_op jit(solution)/shard_map/ppermute | solution.py:21
  39.1 16.9 %collective-permute-start.6 = (bf16[96,3200]{1,0:T(8,128)(2,1)S(1)}, bf16[96,3200]{1,0:T(8,128)(2,1)S(1)}, u32[]{:S(2)}, u32[]{:S(2)}) collective-permute-start(bf16[96,3200]{1,0:T(8,128)(2,1)S(1)} %get-tuple-element.126), channel_id=1, source_target_pairs={{0,32},{32,64},{64,96},{96,0},{1,33},{33,65},{65,97},{97,1},{2,34}... | collective-permute-start | bytes 1843208 | tf_op jit(solution)/shard_map/ppermute | solution.py:21
  60.0 29.0 %all-to-all-start = ((bf16[4,256,896]{2,1,0:T(8,128)(2,1)}), bf16[4,256,896]{2,1,0:T(8,128)(2,1)S(1)}, u32[]{:S(2)}, u32[]{:S(2)}) async-start(bf16[4,256,896]{2,1,0:T(8,128)(2,1)} %shard_map.168), calls=%async_computation | async-start | bytes 3670016 | tf_op jit(solution)/shard_map/all_to_all | solution.py:468
  65.3 21.7 %collective-permute-start.11 = (bf16[96,3200]{1,0:T(8,128)(2,1)S(1)}, bf16[96,3200]{1,0:T(8,128)(2,1)}, u32[]{:S(2)}, u32[]{:S(2)}) collective-permute-start(bf16[96,3200]{1,0:T(8,128)(2,1)S(1)} %copy-done.5), channel_id=1, source_target_pairs={{0,32},{32,64},{64,96},{96,0},{1,33},{33,65},{65,97},{97,1},{2,34}... | collective-permute-start | bytes 1843208 | tf_op jit(solution)/shard_map/ppermute | solution.py:21
  65.8 21.2 %collective-permute-start.12 = (bf16[96,3200]{1,0:T(8,128)(2,1)S(1)}, bf16[96,3200]{1,0:T(8,128)(2,1)}, u32[]{:S(2)}, u32[]{:S(2)}) collective-permute-start(bf16[96,3200]{1,0:T(8,128)(2,1)S(1)} %copy-done.3), channel_id=1, source_target_pairs={{0,96},{32,0},{64,32},{96,64},{1,97},{33,1},{65,33},{97,65},{2,98}... | collective-permute-start | bytes 1843208 | tf_op jit(solution)/shard_map/ppermute | solution.py:21
  68.5 20.4 %collective-permute-start.8 = (bf16[4,384,256]{2,1,0:T(8,128)(2,1)}, bf16[4,384,256]{2,1,0:T(8,128)(2,1)}, u32[]{:S(2)}, u32[]{:S(2)}) collective-permute-start(bf16[4,384,256]{2,1,0:T(8,128)(2,1)} %get-tuple-element.115.refs_3_), channel_id=1, source_target_pairs={{0,16},{8,24},{16,0},{24,8},{1,17},{9,25},{17,1},{25,9},{2,18},{10... | collective-permute-start | bytes 2359304 | tf_op jit(solution)/shard_map/ppermute | solution.py:21
  89.0 18.1 %collective-permute-start.16 = (bf16[4,256,896]{2,1,0:T(8,128)(2,1)S(1)}, bf16[4,256,896]{2,1,0:T(8,128)(2,1)}, u32[]{:S(2)}, u32[]{:S(2)}) collective-permute-start(bf16[4,256,896]{2,1,0:T(8,128)(2,1)S(1)} %all-to-all-done.mine), channel_id=1, source_target_pairs={{0,4},{4,0},{1,5},{5,1},{2,6},{6,2},{3,7},{7,3},{8,12},{12,8},{9,1... | collective-permute-start | bytes 5505032 | tf_op jit(solution)/shard_map/ppermute | solution.py:25
  89.7 17.3 %collective-permute-start.14 = (bf16[96,3200]{1,0:T(8,128)(2,1)}, bf16[96,3200]{1,0:T(8,128)(2,1)S(1)}, u32[]{:S(2)}, u32[]{:S(2)}) collective-permute-start(bf16[96,3200]{1,0:T(8,128)(2,1)} %copy-done.20), channel_id=1, source_target_pairs={{0,32},{32,64},{64,96},{96,0},{1,33},{33,65},{65,97},{97,1},{2,34}... | collective-permute-start | bytes 1843208 | tf_op jit(solution)/shard_map/ppermute | solution.py:21
  90.2 16.8 %collective-permute-start.15 = (bf16[96,3200]{1,0:T(8,128)(2,1)}, bf16[96,3200]{1,0:T(8,128)(2,1)}, u32[]{:S(2)}, u32[]{:S(2)}) collective-permute-start(bf16[96,3200]{1,0:T(8,128)(2,1)} %copy-done.19), channel_id=1, source_target_pairs={{0,96},{32,0},{64,32},{96,64},{1,97},{33,1},{65,33},{97,65},{2,98}... | collective-permute-start | bytes 1843208 | tf_op jit(solution)/shard_map/ppermute | solution.py:21
  118.1 17.5 %collective-permute-start.22 = (bf16[4,384,128]{2,1,0:T(8,128)(2,1)S(1)}, bf16[4,384,128]{2,1,0:T(8,128)(2,1)S(1)}, u32[]{:S(2)}, u32[]{:S(2)}) collective-permute-start(bf16[4,384,128]{2,1,0:T(8,128)(2,1)S(1)} %pad_maximum_fusion.o0), channel_id=1, source_target_pairs={{0,3},{1,0},{2,1},{3,2},{4,7},{5,4},{6,5},{7,6},{8,11},{9,8},{10,9... | collective-permute-start | bytes 1179656 | tf_op jit(solution)/shard_map/ppermute | solution.py:21
  121.2 14.5 %collective-permute-start.21 = (bf16[4,384,128]{2,1,0:T(8,128)(2,1)S(1)}, bf16[4,384,128]{2,1,0:T(8,128)(2,1)S(1)}, u32[]{:S(2)}, u32[]{:S(2)}) collective-permute-start(bf16[4,384,128]{2,1,0:T(8,128)(2,1)S(1)} %pad_maximum_fusion.o0), channel_id=1, source_target_pairs={{0,2},{1,3},{2,0},{3,1},{4,6},{5,7},{6,4},{7,5},{8,10},{9,11},{10,... | collective-permute-start | bytes 1179656 | tf_op jit(solution)/shard_map/ppermute | solution.py:21
  122.0 17.3 %collective-permute-start.20 = (bf16[4,384,128]{2,1,0:T(8,128)(2,1)S(1)}, bf16[4,384,128]{2,1,0:T(8,128)(2,1)S(1)}, u32[]{:S(2)}, u32[]{:S(2)}) collective-permute-start(bf16[4,384,128]{2,1,0:T(8,128)(2,1)S(1)} %pad_maximum_fusion.o0), channel_id=1, source_target_pairs={{0,1},{1,2},{2,3},{3,0},{4,5},{5,6},{6,7},{7,4},{8,9},{9,10},{10,1... | collective-permute-start | bytes 1179656 | tf_op jit(solution)/shard_map/ppermute | solution.py:21
  158.6 14.2 %collective-permute-start.28 = (bf16[96,3200]{1,0:T(8,128)(2,1)}, bf16[96,3200]{1,0:T(8,128)(2,1)S(1)}, u32[]{:S(2)}, u32[]{:S(2)}) collective-permute-start(bf16[96,3200]{1,0:T(8,128)(2,1)} %shard_map.175.refs_0_), channel_id=1, source_target_pairs={{0,24},{8,0},{16,8},{24,16},{1,25},{9,1},{17,9},{25,17},{2,26},{10... | collective-permute-start | bytes 1843208 | tf_op jit(solution)/shard_map/ppermute | solution.py:21
  159.4 15.5 %collective-permute-start.26 = (bf16[96,3200]{1,0:T(8,128)(2,1)}, bf16[96,3200]{1,0:T(8,128)(2,1)S(1)}, u32[]{:S(2)}, u32[]{:S(2)}) collective-permute-start(bf16[96,3200]{1,0:T(8,128)(2,1)} %shard_map.175.refs_0_), channel_id=1, source_target_pairs={{0,8},{8,16},{16,24},{24,0},{1,9},{9,17},{17,25},{25,1},{2,10},{10... | collective-permute-start | bytes 1843208 | tf_op jit(solution)/shard_map/ppermute | solution.py:21
  160.7 14.5 %collective-permute-start.35 = (bf16[512,192]{1,0:T(8,128)(2,1)S(1)}, bf16[512,192]{1,0:T(8,128)(2,1)S(1)}, u32[]{:S(2)}, u32[]{:S(2)}) collective-permute-start(bf16[512,192]{1,0:T(8,128)(2,1)S(1)} %copy.20), channel_id=1, source_target_pairs={{0,0},{1,32},{2,64},{3,96},{32,1},{33,33},{34,65},{35,97},{64,2},{... | collective-permute-start | bytes 589832 | tf_op jit(solution)/shard_map/ppermute | solution.py:516
  161.4 13.7 %collective-permute-start.36 = (f32[1,192]{1,0:T(1,128)S(1)}, f32[1,192]{1,0:T(1,128)S(1)}, u32[]{:S(2)}, u32[]{:S(2)}) collective-permute-start(f32[1,192]{1,0:T(1,128)S(1)} %bitcast.22), channel_id=1, source_target_pairs={{0,0},{1,32},{2,64},{3,96},{32,1},{33,33},{34,65},{35,97},{64,2},{... | collective-permute-start | bytes 2312 | tf_op jit(solution)/shard_map/ppermute | solution.py:517
  162.1 22.0 %collective-permute-start.30 = (bf16[96,3200]{1,0:T(8,128)(2,1)}, bf16[96,3200]{1,0:T(8,128)(2,1)S(1)}, u32[]{:S(2)}, u32[]{:S(2)}) collective-permute-start(bf16[96,3200]{1,0:T(8,128)(2,1)} %shard_map.175.refs_0_), channel_id=1, source_target_pairs={{0,4},{4,0},{1,5},{5,1},{2,6},{6,2},{3,7},{7,3},{8,12},{12,8},{9,1... | collective-permute-start | bytes 1843208 | tf_op jit(solution)/shard_map/ppermute | solution.py:25
  196.7 16.6 %collective-permute-start.38 = (bf16[384,384]{1,0:T(8,128)(2,1)}, bf16[384,384]{1,0:T(8,128)(2,1)S(1)}, u32[]{:S(2)}, u32[]{:S(2)}) collective-permute-start(bf16[384,384]{1,0:T(8,128)(2,1)} %get-tuple-element.177), channel_id=1, source_target_pairs={{0,2},{1,3},{2,0},{3,1},{4,6},{5,7},{6,4},{7,5},{8,10},{9,11},{10,... | collective-permute-start | bytes 884744 | tf_op jit(solution)/shard_map/ppermute | solution.py:21
  199.4 14.1 %collective-permute-start.39 = (bf16[384,384]{1,0:T(8,128)(2,1)}, bf16[384,384]{1,0:T(8,128)(2,1)S(1)}, u32[]{:S(2)}, u32[]{:S(2)}) collective-permute-start(bf16[384,384]{1,0:T(8,128)(2,1)} %get-tuple-element.178), channel_id=1, source_target_pairs={{0,3},{1,0},{2,1},{3,2},{4,7},{5,4},{6,5},{7,6},{8,11},{9,8},{10,9... | collective-permute-start | bytes 884744 | tf_op jit(solution)/shard_map/ppermute | solution.py:21
  218.6 14.5 %collective-permute-start.40 = (bf16[384,384]{1,0:T(8,128)(2,1)S(1)}, bf16[384,384]{1,0:T(8,128)(2,1)S(1)}, u32[]{:S(2)}, u32[]{:S(2)}) collective-permute-start(bf16[384,384]{1,0:T(8,128)(2,1)S(1)} %fusion.2.r0), channel_id=1, source_target_pairs={{0,32},{32,64},{64,96},{96,0},{1,33},{33,65},{65,97},{97,1},{2,34}... | collective-permute-start | bytes 884744 | tf_op jit(solution)/shard_map/ppermute | solution.py:21
  (69 other events, 549.7 us)

commit v2 on v1

--- a/solution.py
+++ b/solution.py
@@ -221,11 +221,11 @@
         return call(
             body,
             [jax.ShapeDtypeStruct((ROWS, HD), BF)] * 4,
-            2.5 * len(steps),
+            (4 if len(steps) == 8 else 2.5 * len(steps)),
             scratch=[pltpu.VMEM(s.shape, s.dtype) for s in state_shapes] + held,
             in_specs=specs,
         )(*args)
-    return call(body, state_shapes, 2.5 * len(steps), scratch=held, in_specs=specs)(*args)
+    return call(body, state_shapes, (4 if len(steps) == 8 else 2.5 * len(steps)), scratch=held, in_specs=specs)(*args)
 
 
 def pack_body(m0, m1, m2, m3, kv_ref, q_ref):
@@ -461,11 +461,12 @@
 
     where = (coords, tile_counts, q_own)
     state = attend((0,) * 4, *where, [kv_own, kv_sib], None, False)
-    near, state, windows, back_low, ahead_high, proj_low, proj_high, kv_here = after(
-        (near, state, windows, back_low, ahead_high, proj_low, proj_high, kv_own)
+    windows, state = after((windows, state))
+    out_half = lax.all_to_all(windows, "z", 0, 0, tiled=True)
+    near, state, back_low, ahead_high, proj_low, proj_high, kv_here = after(
+        (near, state, back_low, ahead_high, proj_low, proj_high, kv_own)
     )
     back_high, ahead_low = shift(proj_high, "y", 1), shift(proj_low, "y", 3)
-    out_half = lax.all_to_all(windows, "z", 0, 0, tiled=True)
     far = shift(kv_here, "x", 2)
     blocks = [near[0], swap(near[0]), near[1], swap(near[1])]
     state = attend((1,) * 4 + (3,) * 4, *where, blocks, state, False)

time: 266 us -> 264 us (level)
  starting transfers between devices: 56.5 us -> 66 us
  Pallas kernels: 89.5 us -> 83.5 us
  waiting for transfers between devices: 98.4 us -> 93.4 us
    ppermute x37, starting transfers between devices: 47.9 us -> 57.2 us  [shift(): return lax.ppermute(value, axis, [(i, (i + k) % 4) for i in range(4)])]
    pallas_call x3, Pallas kernels: 43.2 us -> 37.1 us  [the longest x2 26.1 us: attend(): call(body, state_shapes, 4 if len(steps) == 8 else 2.5 * len(steps), scra...]
    ppermute x37, waiting for transfers between devices: 94.7 us -> 89.4 us  [shift(): return lax.ppermute(value, axis, [(i, (i + k) % 4) for i in range(4)])]
    unnamed x84 -> x74, local copies, waits for them, and re-layouts: 6.82 us -> 5.97 us
  transfers between devices with their start and end apart: 51 -> 51, of which waited for: 31 -> 29; matrix products, arithmetic and copies ran while one was open for 2% -> 2% of each run, Pallas kernels for 18% -> 16%
where the time goes in v2:
time: 264 us
  waiting for transfers between devices  93.4 us (35%)
  Pallas kernels  83.5 us (32%)
  starting transfers between devices  66 us (25%)
  local copies, waits for them, and re-layouts  11 us (4%)
  other arithmetic  8.54 us (3%)
    ppermute x37, waiting for transfers between devices, shift(): return lax.ppermute(value, axis, [(i, (i + k) % 4) for i in range(4)])  89.4 us
    ppermute x37, starting transfers between devices, shift(): return lax.ppermute(value, axis, [(i, (i + k) % 4) for i in range(4)])  57.2 us
    pallas_call x2, Pallas kernels, attend(): call(body, state_shapes, 4 if len(steps) == 8 else 2.5 * len(steps), scra...  26.1 us
    pallas_call x1, Pallas kernels, project_qkv(): pl.pallas_call(qkv_body, out_shape=[jax.ShapeDtypeStruct((ROWS, 3 * HD),...  11.8 us
    pallas_call x1, Pallas kernels, attend(): call(body, [jax.ShapeDtypeStruct((ROWS, HD), BF)] * 4, 4 if len(steps) ==...  10.9 us
    pallas_call x1, Pallas kernels, per_device(): call(projection_body, [jax.ShapeDtypeStruct((ROWS, ROWS), kind) for kind...  9.78 us
    pallas_call x1, Pallas kernels, per_device(): call(out_body, (jax.ShapeDtypeStruct((4, MROWS, share), F32), jax.ShapeDt...  7.31 us
    unnamed x74, local copies, waits for them, and re-layouts  5.97 us
  transfers between devices with their start and end apart: 51, of which 29 were waited for; matrix products, arithmetic and copies ran while one was open for 2% of the time, Pallas kernels for 16%

profile of v2, /device:TPU:0, one launch (start us, length us, event | category | flops | bytes accessed | tf_op | source)
XLA Modules:
  0.0 263.5 jit_solution(9415944587377096317)
XLA Ops:
  1.2 11.8 %shard_map.167 = (bf16[384,384]{1,0:T(8,128)(2,1)}, bf16[384,384]{1,0:T(8,128)(2,1)}, bf16[384,384]{1,0:T(8,128)(2,1)}, bf16[384,384]{1,0:T(8,128)(2,1)}) custom-call(s32[4]{0:T(128)} %pad_add_fusion.s_ref.refs_0_, bf16[384,3200]{1,0:T(8,128)(2,1)} %x_any.1, f32[25,128]{1,0:T(8,128)} %bitcast.20, bf16[3200,512]{1,0:T(8,128)(2,1)} %wk_ref.1, ...), custom_call_target="tpu_custom_call" | custom-call | flops 11000000512 | tf_op jit(solution)/shard_map/pallas_call | solution.py:86
  19.0 3.3 %shard_map.168 = bf16[4,256,896]{2,1,0:T(8,128)(2,1)} custom-call(s32[4]{0:T(128)} %pad_add_fusion.s_ref.refs_0_, bf16[512,3200]{1,0:T(8,128)(2,1)} %w_ref), custom_call_target="tpu_custom_call" | custom-call | flops 100000000 | tf_op jit(solution)/shard_map/pallas_call | solution.py:440
  23.4 7.5 %collective-permute-done.1.m2 = bf16[384,384]{1,0:T(8,128)(2,1)S(1)} collective-permute-done((bf16[384,384]{1,0:T(8,128)(2,1)}, bf16[384,384]{1,0:T(8,128)(2,1)S(1)}, u32[]{:S(2)}, u32[]{:S(2)}) %collective-permute-start.1) | collective-permute-done | bytes 294944 | tf_op jit(solution)/shard_map/ppermute | solution.py:21
  41.5 10.6 %shard_map.170 = (f32[4,384,256]{2,1,0:T(8,128)}, f32[4,384,128]{2,1,0:T(8,128)}) custom-call(s32[4]{0:T(128)} %pad_add_fusion.s_ref.refs_0_, s32[3]{0:T(128)} %refs_1_.5, bf16[4,384,128]{2,1,0:T(8,128)(2,1)} %get-tuple-element.111.refs_2_, bf16[4,384,256]{2,1,0:T(8,128)(2,1)} %get-tuple-element.119.refs_3_, bf16[4,384,256]{2,1,0:T(8,128)(2,1)} %copy-done.14), custom_call_target="tpu_custom_call" | custom-call | flops 10000000000 | tf_op jit(solution)/shard_map/pallas_call | solution.py:228
  52.1 5.4 %all-to-all-start = ((bf16[4,256,896]{2,1,0:T(8,128)(2,1)}), bf16[4,256,896]{2,1,0:T(8,128)(2,1)S(1)}, u32[]{:S(2)}, u32[]{:S(2)}) async-start(bf16[4,256,896]{2,1,0:T(8,128)(2,1)} %shard_map.168), calls=%async_computation | async-start | bytes 3670016 | tf_op jit(solution)/shard_map/all_to_all | solution.py:465
  59.1 7.7 %collective-permute-start.8 = (bf16[4,384,256]{2,1,0:T(8,128)(2,1)S(1)}, bf16[4,384,256]{2,1,0:T(8,128)(2,1)S(1)}, u32[]{:S(2)}, u32[]{:S(2)}) collective-permute-start(bf16[4,384,256]{2,1,0:T(8,128)(2,1)S(1)} %copy-done.12), channel_id=1, source_target_pairs={{0,16},{8,24},{16,0},{24,8},{1,17},{9,25},{17,1},{25,9},{2,18},{10... | collective-permute-start | bytes 2359304 | tf_op jit(solution)/shard_map/ppermute | solution.py:21
  70.1 15.5 %shard_map.171 = (f32[4,384,256]{2,1,0:T(8,128)}, f32[4,384,128]{2,1,0:T(8,128)}) custom-call(s32[4]{0:T(128)} %pad_add_fusion.s_ref.refs_0_, s32[3]{0:T(128)} %refs_1_.5, bf16[4,384,128]{2,1,0:T(8,128)(2,1)} %get-tuple-element.111.refs_2_, bf16[4,384,256]{2,1,0:T(8,128)(2,1)} %collective-permute-done.3.refs_3_, ...), custom_call_target="tpu_custom_call" | custom-call | flops 4000000000 | tf_op jit(solution)/shard_map/pallas_call | solution.py:228
  86.4 3.2 %collective-permute-start.15 = (bf16[96,3200]{1,0:T(8,128)(2,1)}, bf16[96,3200]{1,0:T(8,128)(2,1)}, u32[]{:S(2)}, u32[]{:S(2)}) collective-permute-start(bf16[96,3200]{1,0:T(8,128)(2,1)} %copy-done.15), channel_id=1, source_target_pairs={{0,96},{32,0},{64,32},{96,64},{1,97},{33,1},{65,33},{97,65},{2,98}... | collective-permute-start | bytes 1843208 | tf_op jit(solution)/shard_map/ppermute | solution.py:21
  91.0 10.9 %shard_map.172 = (bf16[384,128]{1,0:T(8,128)(2,1)}, bf16[384,128]{1,0:T(8,128)(2,1)}, bf16[384,128]{1,0:T(8,128)(2,1)}, bf16[384,128]{1,0:T(8,128)(2,1)}) custom-call(s32[4]{0:T(128)} %pad_add_fusion.s_ref.refs_0_, s32[3]{0:T(128)} %refs_1_.5, bf16[4,384,128]{2,1,0:T(8,128)(2,1)} %get-tuple-element.111.refs_2_, bf16[4,384,256]{2,1,0:T(8,128)(2,1)} %copy-done.13, ...), custom_call_target="tpu_custom_call" | custom-call | flops 10000000000 | tf_op jit(solution)/shard_map/pallas_call | solution.py:221
  124.6 7.7 %collective-permute-done.22.o3 = bf16[4,384,128]{2,1,0:T(8,128)(2,1)S(1)} collective-permute-done((bf16[4,384,128]{2,1,0:T(8,128)(2,1)S(1)}, bf16[4,384,128]{2,1,0:T(8,128)(2,1)S(1)}, u32[]{:S(2)}, u32[]{:S(2)}) %collective-permute-start.22) | collective-permute-done | bytes 393248 | tf_op jit(solution)/shard_map/ppermute | solution.py:21
  132.3 3.7 %collective-permute-done.20.o1 = bf16[4,384,128]{2,1,0:T(8,128)(2,1)S(1)} collective-permute-done((bf16[4,384,128]{2,1,0:T(8,128)(2,1)S(1)}, bf16[4,384,128]{2,1,0:T(8,128)(2,1)S(1)}, u32[]{:S(2)}, u32[]{:S(2)}) %collective-permute-start.20) | collective-permute-done | bytes 393248 | tf_op jit(solution)/shard_map/ppermute | solution.py:21
  136.8 7.3 %shard_map.174 = (f32[4,96,800]{2,1,0:T(8,128)}, f32[96,128]{1,0:T(8,128)}) custom-call(s32[4]{0:T(128)} %pad_add_fusion.s_ref.refs_0_, bf16[4,384,128]{2,1,0:T(8,128)(2,1)} %copy-done.2, bf16[4,384,128]{2,1,0:T(8,128)(2,1)} %copy-done.22, bf16[4,384,128]{2,1,0:T(8,128)(2,1)} %copy-done.21, bf16[4,384,128]{2,1,0:T(8,128)(2,1)} %copy-done.20, ...), custom_call_target="tpu_custom_call" | custom-call | flops 6000000000 | tf_op jit(solution)/shard_map/pallas_call | solution.py:496
  159.7 10.3 %collective-permute-done.28.refs_4_ = bf16[96,3200]{1,0:T(8,128)(2,1)S(1)} collective-permute-done((bf16[96,3200]{1,0:T(8,128)(2,1)}, bf16[96,3200]{1,0:T(8,128)(2,1)S(1)}, u32[]{:S(2)}, u32[]{:S(2)}) %collective-permute-start.28) | collective-permute-done | bytes 614432 | tf_op jit(solution)/shard_map/ppermute | solution.py:21
  170.0 3.7 %collective-permute-start.29 = (bf16[48,3200]{1,0:T(8,128)(2,1)S(1)}, bf16[48,3200]{1,0:T(8,128)(2,1)}, u32[]{:S(2)}, u32[]{:S(2)}) collective-permute-start(bf16[48,3200]{1,0:T(8,128)(2,1)S(1)} %slice.41), channel_id=1, source_target_pairs={{0,24},{8,0},{16,8},{24,16},{1,25},{9,1},{17,9},{25,17},{2,26},{10... | collective-permute-start | bytes 921608 | tf_op jit(solution)/shard_map/ppermute | solution.py:21
  174.4 3.7 %collective-permute-done.29.refs_3_ = bf16[48,3200]{1,0:T(8,128)(2,1)} collective-permute-done((bf16[48,3200]{1,0:T(8,128)(2,1)S(1)}, bf16[48,3200]{1,0:T(8,128)(2,1)}, u32[]{:S(2)}, u32[]{:S(2)}) %collective-permute-start.29) | collective-permute-done | bytes 307232 | tf_op jit(solution)/shard_map/ppermute | solution.py:21
  178.1 3.9 %collective-permute-done.27.refs_2_ = bf16[48,3200]{1,0:T(8,128)(2,1)} collective-permute-done((bf16[48,3200]{1,0:T(8,128)(2,1)S(1)}, bf16[48,3200]{1,0:T(8,128)(2,1)}, u32[]{:S(2)}, u32[]{:S(2)}) %collective-permute-start.27) | collective-permute-done | bytes 307232 | tf_op jit(solution)/shard_map/ppermute | solution.py:21
  184.8 9.8 %shard_map.176 = (f32[384,384]{1,0:T(8,128)}, bf16[384,384]{1,0:T(8,128)(2,1)}, bf16[384,384]{1,0:T(8,128)(2,1)}, bf16[384,384]{1,0:T(8,128)(2,1)}) custom-call(s32[4]{0:T(128)} %pad_add_fusion.s_ref.refs_0_, bf16[96,3200]{1,0:T(8,128)(2,1)} %shard_map.175.refs_0_, bf16[96,3200]{1,0:T(8,128)(2,1)} %copy-done.6, ...), custom_call_target="tpu_custom_call" | custom-call | flops 8000000000 | tf_op jit(solution)/shard_map/pallas_call | solution.py:523
  198.9 6.5 %collective-permute-done.37 = bf16[384,384]{1,0:T(8,128)(2,1)S(1)} collective-permute-done((bf16[384,384]{1,0:T(8,128)(2,1)}, bf16[384,384]{1,0:T(8,128)(2,1)S(1)}, u32[]{:S(2)}, u32[]{:S(2)}) %collective-permute-start.37) | collective-permute-done | bytes 294944 | tf_op jit(solution)/shard_map/ppermute | solution.py:21
  205.4 6.6 %collective-permute-done.38 = bf16[384,384]{1,0:T(8,128)(2,1)S(1)} collective-permute-done((bf16[384,384]{1,0:T(8,128)(2,1)}, bf16[384,384]{1,0:T(8,128)(2,1)S(1)}, u32[]{:S(2)}, u32[]{:S(2)}) %collective-permute-start.38) | collective-permute-done | bytes 294944 | tf_op jit(solution)/shard_map/ppermute | solution.py:21
  218.5 6.2 %collective-permute-done.42.r3 = bf16[384,384]{1,0:T(8,128)(2,1)S(1)} collective-permute-done((bf16[384,384]{1,0:T(8,128)(2,1)S(1)}, bf16[384,384]{1,0:T(8,128)(2,1)S(1)}, u32[]{:S(2)}, u32[]{:S(2)}) %collective-permute-start.42) | collective-permute-done | bytes 294944 | tf_op jit(solution)/shard_map/ppermute | solution.py:21
  227.5 4.3 %collective-permute-done.40.r1 = bf16[384,384]{1,0:T(8,128)(2,1)S(1)} collective-permute-done((bf16[384,384]{1,0:T(8,128)(2,1)S(1)}, bf16[384,384]{1,0:T(8,128)(2,1)S(1)}, u32[]{:S(2)}, u32[]{:S(2)}) %collective-permute-start.40) | collective-permute-done | bytes 294944 | tf_op jit(solution)/shard_map/ppermute | solution.py:21
  232.6 4.6 %shard_map.177 = (bf16[448,192]{1,0:T(8,128)(2,1)}, bf16[448,192]{1,0:T(8,128)(2,1)}) custom-call(s32[4]{0:T(128)} %pad_add_fusion.s_ref.refs_0_, bf16[384,384]{1,0:T(8,128)(2,1)} %copy-done.3, bf16[384,384]{1,0:T(8,128)(2,1)} %copy-done.28, bf16[384,384]{1,0:T(8,128)(2,1)} %copy-done.26, bf16[384,384]{1,0:T(8,128)(2,1)} %copy-done.24, ...), custom_call_target="tpu_custom_call" | custom-call | flops 4000000000 | tf_op jit(solution)/shard_map/pallas_call | solution.py:536
  251.2 3.3 %collective-permute-start.49 = (f32[112,128]{1,0:T(8,128)}, f32[112,128]{1,0:T(8,128)S(1)}, u32[]{:S(2)}, u32[]{:S(2)}) collective-permute-start(f32[112,128]{1,0:T(8,128)} %get-tuple-element.189), channel_id=1, source_target_pairs={{0,3},{1,0},{2,1},{3,2},{4,7},{5,4},{6,5},{7,6},{8,11},{9,8},{10,9... | collective-permute-start | bytes 172040 | tf_op jit(solution)/shard_map/ppermute | solution.py:21
  256.6 4.1 %collective-permute-done.48 = f32[112,128]{1,0:T(8,128)S(1)} collective-permute-done((f32[112,128]{1,0:T(8,128)}, f32[112,128]{1,0:T(8,128)S(1)}, u32[]{:S(2)}, u32[]{:S(2)}) %collective-permute-start.48) | collective-permute-done | bytes 57376 | tf_op jit(solution)/shard_map/ppermute | solution.py:21
  (182 shorter events, 100.9 us)
Async XLA Ops:
  14.7 16.2 %collective-permute-start.1 = (bf16[384,384]{1,0:T(8,128)(2,1)}, bf16[384,384]{1,0:T(8,128)(2,1)S(1)}, u32[]{:S(2)}, u32[]{:S(2)}) collective-permute-start(bf16[384,384]{1,0:T(8,128)(2,1)} %get-tuple-element.103), channel_id=1, source_target_pairs={{0,64},{32,96},{64,0},{96,32},{1,65},{33,97},{65,1},{97,33},{2,66}... | collective-permute-start | bytes 884744 | tf_op jit(solution)/shard_map/ppermute | solution.py:21
  17.6 13.3 %collective-permute-start.2 = (bf16[384,384]{1,0:T(8,128)(2,1)}, bf16[384,384]{1,0:T(8,128)(2,1)S(1)}, u32[]{:S(2)}, u32[]{:S(2)}) collective-permute-start(bf16[384,384]{1,0:T(8,128)(2,1)} %get-tuple-element.104), channel_id=1, source_target_pairs={{0,96},{32,0},{64,32},{96,64},{1,97},{33,1},{65,33},{97,65},{2,98}... | collective-permute-start | bytes 884744 | tf_op jit(solution)/shard_map/ppermute | solution.py:21
  34.7 22.9 %collective-permute-start.4 = (bf16[4,384,256]{2,1,0:T(8,128)(2,1)}, bf16[4,384,256]{2,1,0:T(8,128)(2,1)}, u32[]{:S(2)}, u32[]{:S(2)}) collective-permute-start(bf16[4,384,256]{2,1,0:T(8,128)(2,1)} %get-tuple-element.119.refs_3_), channel_id=1, source_target_pairs={{0,24},{8,0},{16,8},{24,16},{1,25},{9,1},{17,9},{25,17},{2,26},{10... | collective-permute-start | bytes 2359304 | tf_op jit(solution)/shard_map/ppermute | solution.py:21
  37.4 21.2 %collective-permute-start.3 = (bf16[4,384,256]{2,1,0:T(8,128)(2,1)}, bf16[4,384,256]{2,1,0:T(8,128)(2,1)}, u32[]{:S(2)}, u32[]{:S(2)}) collective-permute-start(bf16[4,384,256]{2,1,0:T(8,128)(2,1)} %get-tuple-element.119.refs_3_), channel_id=1, source_target_pairs={{0,8},{8,16},{16,24},{24,0},{1,9},{9,17},{17,25},{25,1},{2,10},{10... | collective-permute-start | bytes 2359304 | tf_op jit(solution)/shard_map/ppermute | solution.py:21
  38.6 19.0 %collective-permute-start.7 = (bf16[96,3200]{1,0:T(8,128)(2,1)}, bf16[96,3200]{1,0:T(8,128)(2,1)S(1)}, u32[]{:S(2)}, u32[]{:S(2)}) collective-permute-start(bf16[96,3200]{1,0:T(8,128)(2,1)} %get-tuple-element.129), channel_id=1, source_target_pairs={{0,96},{32,0},{64,32},{96,64},{1,97},{33,1},{65,33},{97,65},{2,98}... | collective-permute-start | bytes 1843208 | tf_op jit(solution)/shard_map/ppermute | solution.py:21
  40.0 17.6 %collective-permute-start.6 = (bf16[96,3200]{1,0:T(8,128)(2,1)}, bf16[96,3200]{1,0:T(8,128)(2,1)}, u32[]{:S(2)}, u32[]{:S(2)}) collective-permute-start(bf16[96,3200]{1,0:T(8,128)(2,1)} %get-tuple-element.130), channel_id=1, source_target_pairs={{0,32},{32,64},{64,96},{96,0},{1,33},{33,65},{65,97},{97,1},{2,34}... | collective-permute-start | bytes 1843208 | tf_op jit(solution)/shard_map/ppermute | solution.py:21
  52.1 33.5 %all-to-all-start = ((bf16[4,256,896]{2,1,0:T(8,128)(2,1)}), bf16[4,256,896]{2,1,0:T(8,128)(2,1)S(1)}, u32[]{:S(2)}, u32[]{:S(2)}) async-start(bf16[4,256,896]{2,1,0:T(8,128)(2,1)} %shard_map.168), calls=%async_computation | async-start | bytes 3670016 | tf_op jit(solution)/shard_map/all_to_all | solution.py:465
  59.1 26.4 %collective-permute-start.8 = (bf16[4,384,256]{2,1,0:T(8,128)(2,1)S(1)}, bf16[4,384,256]{2,1,0:T(8,128)(2,1)S(1)}, u32[]{:S(2)}, u32[]{:S(2)}) collective-permute-start(bf16[4,384,256]{2,1,0:T(8,128)(2,1)S(1)} %copy-done.12), channel_id=1, source_target_pairs={{0,16},{8,24},{16,0},{24,8},{1,17},{9,25},{17,1},{25,9},{2,18},{10... | collective-permute-start | bytes 2359304 | tf_op jit(solution)/shard_map/ppermute | solution.py:21
  66.8 18.8 %collective-permute-start.11 = (bf16[96,3200]{1,0:T(8,128)(2,1)}, bf16[96,3200]{1,0:T(8,128)(2,1)}, u32[]{:S(2)}, u32[]{:S(2)}) collective-permute-start(bf16[96,3200]{1,0:T(8,128)(2,1)} %get-tuple-element.129), channel_id=1, source_target_pairs={{0,32},{32,64},{64,96},{96,0},{1,33},{33,65},{65,97},{97,1},{2,34}... | collective-permute-start | bytes 1843208 | tf_op jit(solution)/shard_map/ppermute | solution.py:21
  67.3 18.3 %collective-permute-start.12 = (bf16[96,3200]{1,0:T(8,128)(2,1)}, bf16[96,3200]{1,0:T(8,128)(2,1)}, u32[]{:S(2)}, u32[]{:S(2)}) collective-permute-start(bf16[96,3200]{1,0:T(8,128)(2,1)} %get-tuple-element.130), channel_id=1, source_target_pairs={{0,96},{32,0},{64,32},{96,64},{1,97},{33,1},{65,33},{97,65},{2,98}... | collective-permute-start | bytes 1843208 | tf_op jit(solution)/shard_map/ppermute | solution.py:21
  85.7 18.1 %collective-permute-start.16 = (bf16[4,256,896]{2,1,0:T(8,128)(2,1)S(1)}, bf16[4,256,896]{2,1,0:T(8,128)(2,1)}, u32[]{:S(2)}, u32[]{:S(2)}) collective-permute-start(bf16[4,256,896]{2,1,0:T(8,128)(2,1)S(1)} %all-to-all-done.mine), channel_id=1, source_target_pairs={{0,4},{4,0},{1,5},{5,1},{2,6},{6,2},{3,7},{7,3},{8,12},{12,8},{9,1... | collective-permute-start | bytes 5505032 | tf_op jit(solution)/shard_map/ppermute | solution.py:25
  86.4 17.3 %collective-permute-start.14 = (bf16[96,3200]{1,0:T(8,128)(2,1)}, bf16[96,3200]{1,0:T(8,128)(2,1)S(1)}, u32[]{:S(2)}, u32[]{:S(2)}) collective-permute-start(bf16[96,3200]{1,0:T(8,128)(2,1)} %collective-permute-done.6.refs_11_), channel_id=1, source_target_pairs={{0,32},{32,64},{64,96},{96,0},{1,33},{33,65},{65,97},{97,1},{2,34}... | collective-permute-start | bytes 1843208 | tf_op jit(solution)/shard_map/ppermute | solution.py:21
  86.4 17.3 %collective-permute-start.15 = (bf16[96,3200]{1,0:T(8,128)(2,1)}, bf16[96,3200]{1,0:T(8,128)(2,1)}, u32[]{:S(2)}, u32[]{:S(2)}) collective-permute-start(bf16[96,3200]{1,0:T(8,128)(2,1)} %copy-done.15), channel_id=1, source_target_pairs={{0,96},{32,0},{64,32},{96,64},{1,97},{33,1},{65,33},{97,65},{2,98}... | collective-permute-start | bytes 1843208 | tf_op jit(solution)/shard_map/ppermute | solution.py:21
  114.8 17.5 %collective-permute-start.22 = (bf16[4,384,128]{2,1,0:T(8,128)(2,1)S(1)}, bf16[4,384,128]{2,1,0:T(8,128)(2,1)S(1)}, u32[]{:S(2)}, u32[]{:S(2)}) collective-permute-start(bf16[4,384,128]{2,1,0:T(8,128)(2,1)S(1)} %pad_maximum_fusion.o0), channel_id=1, source_target_pairs={{0,3},{1,0},{2,1},{3,2},{4,7},{5,4},{6,5},{7,6},{8,11},{9,8},{10,9... | collective-permute-start | bytes 1179656 | tf_op jit(solution)/shard_map/ppermute | solution.py:21
  117.8 14.5 %collective-permute-start.21 = (bf16[4,384,128]{2,1,0:T(8,128)(2,1)S(1)}, bf16[4,384,128]{2,1,0:T(8,128)(2,1)S(1)}, u32[]{:S(2)}, u32[]{:S(2)}) collective-permute-start(bf16[4,384,128]{2,1,0:T(8,128)(2,1)S(1)} %pad_maximum_fusion.o0), channel_id=1, source_target_pairs={{0,2},{1,3},{2,0},{3,1},{4,6},{5,7},{6,4},{7,5},{8,10},{9,11},{10,... | collective-permute-start | bytes 1179656 | tf_op jit(solution)/shard_map/ppermute | solution.py:21
  118.7 17.3 %collective-permute-start.20 = (bf16[4,384,128]{2,1,0:T(8,128)(2,1)S(1)}, bf16[4,384,128]{2,1,0:T(8,128)(2,1)S(1)}, u32[]{:S(2)}, u32[]{:S(2)}) collective-permute-start(bf16[4,384,128]{2,1,0:T(8,128)(2,1)S(1)} %pad_maximum_fusion.o0), channel_id=1, source_target_pairs={{0,1},{1,2},{2,3},{3,0},{4,5},{5,6},{6,7},{7,4},{8,9},{9,10},{10,1... | collective-permute-start | bytes 1179656 | tf_op jit(solution)/shard_map/ppermute | solution.py:21
  155.3 14.7 %collective-permute-start.28 = (bf16[96,3200]{1,0:T(8,128)(2,1)}, bf16[96,3200]{1,0:T(8,128)(2,1)S(1)}, u32[]{:S(2)}, u32[]{:S(2)}) collective-permute-start(bf16[96,3200]{1,0:T(8,128)(2,1)} %shard_map.175.refs_0_), channel_id=1, source_target_pairs={{0,24},{8,0},{16,8},{24,16},{1,25},{9,1},{17,9},{25,17},{2,26},{10... | collective-permute-start | bytes 1843208 | tf_op jit(solution)/shard_map/ppermute | solution.py:21
  158.1 15.6 %collective-permute-start.26 = (bf16[96,3200]{1,0:T(8,128)(2,1)}, bf16[96,3200]{1,0:T(8,128)(2,1)S(1)}, u32[]{:S(2)}, u32[]{:S(2)}) collective-permute-start(bf16[96,3200]{1,0:T(8,128)(2,1)} %shard_map.175.refs_0_), channel_id=1, source_target_pairs={{0,8},{8,16},{16,24},{24,0},{1,9},{9,17},{17,25},{25,1},{2,10},{10... | collective-permute-start | bytes 1843208 | tf_op jit(solution)/shard_map/ppermute | solution.py:21
  158.2 15.7 %collective-permute-start.35 = (bf16[512,192]{1,0:T(8,128)(2,1)S(1)}, bf16[512,192]{1,0:T(8,128)(2,1)S(1)}, u32[]{:S(2)}, u32[]{:S(2)}) collective-permute-start(bf16[512,192]{1,0:T(8,128)(2,1)S(1)} %copy.20), channel_id=1, source_target_pairs={{0,0},{1,32},{2,64},{3,96},{32,1},{33,33},{34,65},{35,97},{64,2},{... | collective-permute-start | bytes 589832 | tf_op jit(solution)/shard_map/ppermute | solution.py:517
  158.9 14.9 %collective-permute-start.36 = (f32[1,192]{1,0:T(1,128)S(1)}, f32[1,192]{1,0:T(1,128)S(1)}, u32[]{:S(2)}, u32[]{:S(2)}) collective-permute-start(f32[1,192]{1,0:T(1,128)S(1)} %bitcast.22), channel_id=1, source_target_pairs={{0,0},{1,32},{2,64},{3,96},{32,1},{33,33},{34,65},{35,97},{64,2},{... | collective-permute-start | bytes 2312 | tf_op jit(solution)/shard_map/ppermute | solution.py:518
  159.6 23.2 %collective-permute-start.30 = (bf16[96,3200]{1,0:T(8,128)(2,1)}, bf16[96,3200]{1,0:T(8,128)(2,1)S(1)}, u32[]{:S(2)}, u32[]{:S(2)}) collective-permute-start(bf16[96,3200]{1,0:T(8,128)(2,1)} %shard_map.175.refs_0_), channel_id=1, source_target_pairs={{0,4},{4,0},{1,5},{5,1},{2,6},{6,2},{3,7},{7,3},{8,12},{12,8},{9,1... | collective-permute-start | bytes 1843208 | tf_op jit(solution)/shard_map/ppermute | solution.py:25
  195.4 16.6 %collective-permute-start.38 = (bf16[384,384]{1,0:T(8,128)(2,1)}, bf16[384,384]{1,0:T(8,128)(2,1)S(1)}, u32[]{:S(2)}, u32[]{:S(2)}) collective-permute-start(bf16[384,384]{1,0:T(8,128)(2,1)} %get-tuple-element.181), channel_id=1, source_target_pairs={{0,2},{1,3},{2,0},{3,1},{4,6},{5,7},{6,4},{7,5},{8,10},{9,11},{10,... | collective-permute-start | bytes 884744 | tf_op jit(solution)/shard_map/ppermute | solution.py:21
  198.1 14.1 %collective-permute-start.39 = (bf16[384,384]{1,0:T(8,128)(2,1)}, bf16[384,384]{1,0:T(8,128)(2,1)S(1)}, u32[]{:S(2)}, u32[]{:S(2)}) collective-permute-start(bf16[384,384]{1,0:T(8,128)(2,1)} %get-tuple-element.182), channel_id=1, source_target_pairs={{0,3},{1,0},{2,1},{3,2},{4,7},{5,4},{6,5},{7,6},{8,11},{9,8},{10,9... | collective-permute-start | bytes 884744 | tf_op jit(solution)/shard_map/ppermute | solution.py:21
  217.2 14.7 %collective-permute-start.40 = (bf16[384,384]{1,0:T(8,128)(2,1)S(1)}, bf16[384,384]{1,0:T(8,128)(2,1)S(1)}, u32[]{:S(2)}, u32[]{:S(2)}) collective-permute-start(bf16[384,384]{1,0:T(8,128)(2,1)S(1)} %fusion.2.r0), channel_id=1, source_target_pairs={{0,32},{32,64},{64,96},{96,0},{1,33},{33,65},{65,97},{97,1},{2,34}... | collective-permute-start | bytes 884744 | tf_op jit(solution)/shard_map/ppermute | solution.py:21
  (64 other events, 518.7 us)
